TPU v7x, 128 devices: a whole 4x4x4 slice. The times are simulated.
128 devices in a mesh: tm: 32 (over z, y, core), obs: 4 (over x).
Axes of the slice: x: 4, y: 4, z: 4, core: 2. Of those that a mesh axis runs over, the one named last changes fastest.
Arguments:
- records: bfloat16 [524288, 512], P(('tm', 'obs')), may hold values from -0.25 to 0.25
- obs_values: bfloat16 [524288], P(('tm', 'obs')), may hold values from -18 to 18
- block_day: int32 [4096], P(('tm', 'obs')), may hold values from 0 to 1
- block_count: int32 [4096], P(('tm', 'obs')), may hold values from 1 to 128
- propagator_matrix: float32 [512, 512], replicated, may hold values from -1 to 1
- analysis_cov: float32 [512, 512], replicated, may hold values from -0.05 to 0.1, as said below
- unattenuated_multiplier: float32 [512, 512], P('obs'), may hold values from -0.3 to 1
- damping: float32 [64, 512], P('tm'), may hold values from 0 to 1
- prior_mean: float32 [512], P('obs'), may hold values from -6 to 6
Outputs:
- filtered: float32 [64, 512], P('tm', 'obs')
- smoothed: float32 [64, 512], P('tm', 'obs')
Inputs may be any that keep to these rules, and one draw needn't show every extreme that they name: `analysis_cov`: Symmetric.
All inputs are finite; a program needn't handle non-finite values.
Results may differ from a plain program's by a relative error of at most 0.0003.
Values may be sent and summed in bfloat16 or wider, within the bound.
A program may use at most 192 MiB of HBM per device.

v0:
```python
import jax
import jax.numpy as jnp
from jax import lax
from jax.sharding import PartitionSpec as P


def carried_in(x, axis, combine, identity, reverse):
    peers, position = (lax.axis_size(axis), lax.axis_index(axis))
    everything = jax.tree.map(lambda part: lax.all_gather(part, axis), x)
    start = jax.tree.map(
        lambda part, zero: jnp.broadcast_to(jnp.asarray(zero, part.dtype), part.shape), x, identity
    )

    def lap(k, before):
        at = peers - 1 - k if reverse else k
        reached = at > position if reverse else at < position
        new = combine(before, jax.tree.map(lambda part: part[at], everything))
        return jax.tree.map(lambda a, b: jnp.where(reached, a, b), new, before)

    return lax.fori_loop(0, peers, lap, start)


def from_behind(x, axis, by):
    peers = lax.axis_size(axis)
    pairs = [(i, i + by) for i in range(peers) if 0 <= i + by < peers]
    return lax.ppermute(x, axis, pairs)


def day_grams(rows_all, values_all, days_of_block, counts_of_block, day_total):
    maximal_accuracy = lax.Precision.HIGHEST
    block_total = days_of_block.shape[0]
    slot_total = rows_all.shape[0] // block_total
    width = rows_all.shape[1]
    slot_index = lax.broadcasted_iota(jnp.int32, (block_total, slot_total), 1)
    valid_mask = slot_index < counts_of_block[:, None]
    nothing = jnp.zeros((), rows_all.dtype)
    held_rows = jnp.where(
        valid_mask[:, :, None], rows_all.reshape(block_total, slot_total, width), nothing
    )
    held_values = jnp.where(valid_mask, values_all.reshape(block_total, slot_total), nothing)
    day_mark = (
        days_of_block[:, None] == lax.broadcasted_iota(jnp.int32, (block_total, day_total), 1)
    ).astype(jnp.float32)
    block_info = jnp.einsum(
        "bk,bks->bs", held_values, held_rows, preferred_element_type=jnp.float32
    )
    info = jnp.einsum("bd,bs->ds", day_mark, block_info, precision=maximal_accuracy)

    def one_day(day_number):
        chosen = (days_of_block == day_number)[:, None, None]
        picked = jnp.where(chosen, held_rows, nothing).reshape(block_total * slot_total, width)
        return lax.dot_general(
            picked, picked, (((0,), (0,)), ((), ())), preferred_element_type=jnp.float32
        )

    omega = lax.map(one_day, jnp.arange(day_total, dtype=jnp.int32))
    return (omega, info)


def fold_rows(left_rows, running, pieces):
    maximal_accuracy = lax.Precision.HIGHEST
    return (
        jnp.dot(left_rows, pieces[0], precision=maximal_accuracy),
        running[1] + jnp.dot(left_rows, pieces[1], precision=maximal_accuracy),
    )


def compose(earlier, subsequent_dates):
    maximal_accuracy = lax.Precision.HIGHEST
    return (
        jnp.dot(subsequent_dates[0], earlier[0], precision=maximal_accuracy),
        jnp.dot(subsequent_dates[0], earlier[1], precision=maximal_accuracy) + subsequent_dates[1],
    )


def local(
    records,
    obs_values,
    block_day,
    block_count,
    propagator_matrix,
    analysis_cov,
    unattenuated_multiplier,
    damping,
    prior_mean,
):
    maximal_accuracy = lax.Precision.HIGHEST
    width = propagator_matrix.shape[0]
    row_count = prior_mean.shape[0]
    day_count = damping.shape[0]
    first_row = lax.axis_index("obs") * row_count
    got_rows, got_values, got_days, got_counts = (
        lax.all_to_all(records, "tm", split_axis=0, concat_axis=0, tiled=True),
        lax.all_to_all(obs_values, "tm", split_axis=0, concat_axis=0, tiled=True),
        lax.all_to_all(block_day, "tm", split_axis=0, concat_axis=0, tiled=True),
        lax.all_to_all(block_count, "tm", split_axis=0, concat_axis=0, tiled=True),
    )
    omega_part, info_part = day_grams(got_rows, got_values, got_days, got_counts, day_count)
    trans_rows = lax.dynamic_slice_in_dim(propagator_matrix, first_row, row_count, 0)
    damp_rows = lax.dynamic_slice_in_dim(damping, first_row, row_count, 1)
    moved_rows = damp_rows[:, :, None] * trans_rows[None, :, :]
    omega, info = lax.psum((omega_part, info_part), "obs")
    cov_rows = lax.dynamic_slice_in_dim(analysis_cov, first_row, row_count, 0)
    weighted = jnp.einsum("rs,dst->drt", cov_rows, omega, precision=maximal_accuracy)
    correction = jnp.einsum(
        "drs,st->drt", weighted * damping[:, None, :], propagator_matrix, precision=maximal_accuracy
    )
    shift_rows = jnp.einsum("bt,ft->fb", cov_rows, info, precision=maximal_accuracy)
    step_rows = moved_rows - correction

    def forward_day(day_index, stacks):
        products, offsets = stacks
        left_rows = lax.dynamic_index_in_dim(step_rows, day_index, 0, keepdims=False)
        previous = (
            lax.dynamic_index_in_dim(products, day_index - 1, 0, keepdims=False),
            lax.dynamic_index_in_dim(offsets, day_index - 1, 0, keepdims=False),
        )
        initial = (
            jnp.zeros((row_count, width), jnp.float32),
            lax.dynamic_index_in_dim(shift_rows, day_index, 0, keepdims=False),
        )
        new_map, new_offset = fold_rows(
            left_rows,
            initial,
            (
                lax.all_gather(previous[0], "obs", axis=0, tiled=True),
                lax.all_gather(previous[1], "obs", axis=0, tiled=True),
            ),
        )
        return (products.at[day_index].set(new_map), offsets.at[day_index].set(new_offset))

    products, offsets = lax.fori_loop(1, day_count, forward_day, (step_rows, shift_rows))
    full_map, full_offset, prior_full = (
        lax.all_gather(products[day_count - 1], "obs", axis=0, tiled=True),
        lax.all_gather(offsets[day_count - 1], "obs", axis=0, tiled=True),
        lax.all_gather(prior_mean, "obs", axis=0, tiled=True),
    )
    identity = jnp.eye(width, dtype=jnp.float32)
    before_map, before_offset = carried_in(
        (full_map, full_offset), "tm", compose, (identity, jnp.zeros((width,), jnp.float32)), False
    )
    start_state = jnp.dot(before_map, prior_full, precision=maximal_accuracy) + before_offset
    filt_rows = jnp.einsum("drs,s->dr", products, start_state, precision=maximal_accuracy) + offsets
    filtered_whole = lax.all_gather(filt_rows, "obs", axis=1, tiled=True)
    next_first = from_behind(damping[0:1], "tm", -1)
    attenuated_successor = jnp.concatenate([damping[1:], next_first], 0)
    predicted_vector = attenuated_successor * jnp.einsum(
        "ef,qf->eq", filtered_whole, propagator_matrix, precision=maximal_accuracy
    )
    gain_rows = unattenuated_multiplier[None, :, :] * attenuated_successor[:, None, :]
    const_rows = filt_rows - jnp.einsum(
        "bt,ft->fb",
        unattenuated_multiplier,
        attenuated_successor * predicted_vector,
        precision=maximal_accuracy,
    )

    def backward_day(step_index, stacks):
        chains, consts = stacks
        day_index = day_count - 2 - step_index
        left_rows = lax.dynamic_index_in_dim(gain_rows, day_index, 0, keepdims=False)
        previous = (
            lax.dynamic_index_in_dim(chains, day_index + 1, 0, keepdims=False),
            lax.dynamic_index_in_dim(consts, day_index + 1, 0, keepdims=False),
        )
        initial = (
            jnp.zeros((row_count, width), jnp.float32),
            lax.dynamic_index_in_dim(const_rows, day_index, 0, keepdims=False),
        )
        new_map, new_offset = fold_rows(
            left_rows,
            initial,
            (
                lax.all_gather(previous[0], "obs", axis=0, tiled=True),
                lax.all_gather(previous[1], "obs", axis=0, tiled=True),
            ),
        )
        return (chains.at[day_index].set(new_map), consts.at[day_index].set(new_offset))

    chains, consts = lax.fori_loop(0, day_count - 1, backward_day, (gain_rows, const_rows))
    back_map, back_offset = (
        lax.all_gather(chains[0], "obs", axis=0, tiled=True),
        lax.all_gather(consts[0], "obs", axis=0, tiled=True),
    )
    identity_back = jnp.eye(width, dtype=jnp.float32)
    _, after_offset = carried_in(
        (back_map, back_offset),
        "tm",
        compose,
        (identity_back, jnp.zeros((width,), jnp.float32)),
        True,
    )
    smooth_rows = jnp.einsum("drs,s->dr", chains, after_offset, precision=maximal_accuracy) + consts
    return (filt_rows, smooth_rows)


def solution(mesh):
    return jax.shard_map(
        local,
        mesh=mesh,
        in_specs=(
            P(("tm", "obs"), None),
            P(("tm", "obs")),
            P(("tm", "obs")),
            P(("tm", "obs")),
            P(),
            P(),
            P("obs", None),
            P("tm", None),
            P("obs"),
        ),
        out_specs=(P("tm", "obs"), P("tm", "obs")),
        check_vma=False,
    )
```

profile of v0, /device:TPU:1, one launch (start us, length us, event | category | flops | bytes accessed | tf_op | source)
XLA Modules:
  0.0 713.3 jit_solution(17349730037595241578)
XLA Ops:
  8.6 9.6 %all-to-all-start = ((s32[32,1,1]{2,1,0:T(1,128)}), s32[32,1,1]{2,1,0:T(1,128)S(1)}, u32[]{:S(2)}, u32[]{:S(2)}) async-start(s32[32,1,1]{2,1,0:T(1,128)} %copy.25), calls=%async_computation | async-start | bytes 32768 | tf_op jit(solution)/shard_map/all_to_all | solution.py:95
  19.0 6.2 all-to-all-done
  25.2 10.7 %all_to_all.39 = s32[32,1,1]{2,1,0:T(1,128)S(1)} all-to-all(s32[32,1,1]{2,1,0:T(1,128)S(1)} %copy.26), channel_id=1, replica_groups=mesh['tm'=32,'obs'=4] {'tm'}, dimensions={0} | all-to-all | bytes 256 | tf_op jit(solution)/shard_map/all_to_all | solution.py:96
  35.8 5.1 all-to-all-start.2
  42.4 48.9 %all-to-all-done.2 = bf16[32,128,512]{2,1,0:T(8,128)(2,1)} async-done(((bf16[32,128,512]{2,1,0:T(8,128)(2,1)}), bf16[32,128,512]{2,1,0:T(8,128)(2,1)}, u32[]{:S(2)}, u32[]{:S(2)}) %all-to-all-start.2) | async-done | bytes 4194336 | tf_op jit(solution)/shard_map/all_to_all | solution.py:93
  91.3 3.9 broadcast_select_fusion.2
  95.2 6.4 copy.27
  101.7 14.3 %while.58 = (s32[]{:T(128)}, f32[2,512,512]{1,2,0:T(8,128)S(1)}, s32[2]{0:T(128)S(1)}, s32[32]{0:T(128)S(1)}, bf16[32,128,512]{1,2,0:T(8,128)(2,1)}, /*index=5*/s32[]{:T(128)}) while((s32[]{:T(128)}, f32[2,512,512]{1,2,0:T(8,128)S(1)}, s32[2]{0:T(128)S(1)}, s32[32]{0:T(128)S(1)}, bf16[32,128,512]{1,2,0:T(8,128)(2,1)}, ...), condition=%wide.region_1.2_spmd, body=%wide.region_0.1_spmd.sunk | while | flops 2149580800 | bytes 5243649 | solution.py:56
  102.9 5.9 fusion.79
  110.1 5.9 fusion.79
  117.5 58.3 %all-reduce.2.cloned.1.call-done = f32[2,512,512]{1,2,0:T(8,128)} async-done(((f32[2,512,512]{1,2,0:T(8,128)}), f32[2,512,512]{1,2,0:T(8,128)}) %all-reduce.2.cloned.1.call-update) | async-done | bytes 2097168 | tf_op jit(solution)/shard_map/psum | solution.py:102
  175.8 3.4 fusion.22
  186.9 17.0 %all-gather.24.cloned.1.call-done = f32[1,512,512]{2,1,0:T(8,128)} async-done(((f32[1,128,512]{2,1,0:T(8,128)}), f32[1,512,512]{2,1,0:T(8,128)}) %all-gather.24.cloned.1.call-update) | async-done | bytes 1048592 | tf_op jit(solution)/shard_map/while/body/eval_jaxpr/all_gather | solution.py:126
  206.7 23.4 %all-gather.28.cloned.1.call-done = f32[1,512,512]{2,1,0:T(8,128)} async-done(((f32[1,128,512]{2,1,0:T(8,128)}), f32[1,512,512]{2,1,0:T(8,128)}) %all-gather.28.cloned.1.call-update) | async-done | bytes 1048592 | tf_op jit(solution)/shard_map/while/body/eval_jaxpr/all_gather | solution.py:174
  232.8 23.2 %all-gather.20.cloned.1.call-done = f32[512,512]{1,0:T(8,128)} async-done(((f32[128,512]{1,0:T(8,128)}), f32[512,512]{1,0:T(8,128)}) %all-gather.20.cloned.1.call-update) | async-done | bytes 1048592 | tf_op jit(solution)/shard_map/all_gather | solution.py:134
  256.0 25.8 %all-gather.22.cloned.1.call-done = f32[512,512]{1,0:T(8,128)} async-done(((f32[128,512]{1,0:T(8,128)}), f32[512,512]{1,0:T(8,128)}) %all-gather.22.cloned.1.call-update) | async-done | bytes 1048592 | tf_op jit(solution)/shard_map/all_gather | solution.py:182
  282.5 8.6 %all-to-all-start.3 = ((bf16[32,128,1]{1,2,0:T(2,128)(2,1)}), bf16[32,128,1]{1,2,0:T(2,128)(2,1)S(1)}, u32[]{:S(2)}, u32[]{:S(2)}) async-start(bf16[32,128,1]{1,2,0:T(2,128)(2,1)} %copy.30), calls=%async_computation.3 | async-start | bytes 32768 | tf_op jit(solution)/shard_map/all_to_all | solution.py:94
  291.3 6.7 all-gather.10
  301.3 8.6 %psum.15 = f32[2,512]{1,0:T(2,128)S(1)} all-reduce(f32[2,512]{1,0:T(2,128)S(1)} %fusion.36), channel_id=1, replica_groups=mesh['tm'=32,'obs'=4] {'obs'}, use_global_device_ids=true, to_apply=%region_3.4 | all-reduce | flops 1024 | bytes 8192 | tf_op jit(solution)/shard_map/psum | solution.py:102
  311.1 6.0 all-gather.2
  317.4 6.7 all-gather.8
  324.1 29.3 %all-gather.9 = f32[32,1,512]{2,1,0:T(1,128)S(1)} all-gather(f32[1,1,512]{2,1,0:T(1,128)S(1)} %bitcast.166), channel_id=5, replica_groups=mesh['tm'=32,'obs'=4] {'tm'}, dimensions={0}, use_global_device_ids=true | all-gather | bytes 67584 | tf_op jit(solution)/shard_map/all_gather | solution.py:9
  353.6 46.5 %all-gather.26.cloned.1.call-done = f32[16384,512]{1,0:T(8,128)} async-done(((f32[512,512]{1,0:T(8,128)}), f32[16384,512]{1,0:T(8,128)}) %all-gather.26.cloned.1.call-update) | async-done | bytes 33554448 | tf_op jit(solution)/shard_map/all_gather | solution.py:9
  400.1 175.1 %while.59 = (s32[]{:T(128)}, f32[512,512]{1,0:T(8,128)S(1)}, f32[512]{0:T(512)S(1)}, s32[]{:T(128)}, f32[32,512,512]{2,1,0:T(8,128)}, /*index=5*/f32[32,512]{1,0:T(8,128)S(1)}, s32[]{:T(128)}, s32[]{:T(128)}) while((s32[]{:T(128)}, f32[512,512]{1,0:T(8,128)S(1)}, f32[512]{0:T(512)S(1)}, s32[]{:T(128)}, f32[32,512,512]{2,1,0:T(8,128)}, ...), condition=%wide.region_5.6_spmd.clone, body=%wide.region_4.5_spmd.clone.sunk | while | flops 1614022656 | bytes 7360639 | solution.py:20
  411.0 3.2 convolution_select_fusion.2
  422.1 3.1 convolution_select_fusion.2
  427.6 3.1 convolution_select_fusion.2
  577.8 7.7 %all_gather.71 = f32[2,512]{1,0:T(2,128)S(1)} all-gather(f32[2,128]{1,0:T(2,128)S(1)} %add.145), channel_id=1, replica_groups=mesh['tm'=32,'obs'=4] {'obs'}, dimensions={1}, use_global_device_ids=true | all-gather | bytes 5120 | tf_op jit(solution)/shard_map/all_gather | solution.py:144
  587.7 5.2 all-gather.6
  594.1 6.7 all-gather.11
  600.8 30.5 %all-gather.12 = f32[32,1,512]{2,1,0:T(1,128)S(1)} all-gather(f32[1,1,512]{2,1,0:T(1,128)S(1)} %bitcast.167), channel_id=9, replica_groups=mesh['tm'=32,'obs'=4] {'tm'}, dimensions={0}, use_global_device_ids=true | all-gather | bytes 67584 | tf_op jit(solution)/shard_map/all_gather | solution.py:9
  632.1 73.2 %while.60 = (s32[]{:T(128)}, f32[512]{0:T(512)S(1)}, s32[]{:T(128)}, f32[32,512,512]{2,1,0:T(8,128)}, f32[32,512]{1,0:T(8,128)S(1)}, /*index=5*/s32[]{:T(128)}, s32[]{:T(128)}, s32[]{:T(128)}, s32[]{:T(128)}) while((s32[]{:T(128)}, f32[512]{0:T(512)S(1)}, s32[]{:T(128)}, f32[32,512,512]{2,1,0:T(8,128)}, f32[32,512]{1,0:T(8,128)S(1)}, ...), condition=%wide.region_7.8_spmd.clone, body=%wide.region_6.7_spmd.clone.sunk | while | flops 3147784 | bytes 1069232 | solution.py:20
  (406 shorter events, 269.7 us)
Async XLA Ops:
  7.2 110.3 %copy-start = (f32[512,512]{1,0:T(8,128)S(1)}, f32[512,512]{1,0:T(8,128)}, u32[]{:S(2)}) copy-start(f32[512,512]{1,0:T(8,128)} %param.27) | copy-start | bytes 3145732
  8.6 16.5 %all-to-all-start = ((s32[32,1,1]{2,1,0:T(1,128)}), s32[32,1,1]{2,1,0:T(1,128)S(1)}, u32[]{:S(2)}, u32[]{:S(2)}) async-start(s32[32,1,1]{2,1,0:T(1,128)} %copy.25), calls=%async_computation | async-start | bytes 32768 | tf_op jit(solution)/shard_map/all_to_all | solution.py:95
  35.8 55.5 %all-to-all-start.2 = ((bf16[32,128,512]{2,1,0:T(8,128)(2,1)}), bf16[32,128,512]{2,1,0:T(8,128)(2,1)}, u32[]{:S(2)}, u32[]{:S(2)}) async-start(bf16[32,128,512]{2,1,0:T(8,128)(2,1)} %bitcast.151), calls=%async_computation.2 | async-start | bytes 8388608 | tf_op jit(solution)/shard_map/all_to_all | solution.py:93
  40.9 134.9 %all-reduce.2.cloned.1.call-start = ((), (), s32[]{:S(2)}) async-start(), calls=%async_computation.4 | async-start | bytes 4194304 | tf_op jit(solution)/shard_map/psum | solution.py:102
  101.6 15.7 %copy-start.8 = (f32[2,512]{1,0:T(2,128)S(1)}, f32[2,512]{1,0:T(2,128)}, u32[]{:S(2)}) copy-start(f32[2,512]{1,0:T(2,128)} %param.30) | copy-start | bytes 12292
  116.0 1.3 copy-start.6
  116.0 70.0 %copy-start.7 = (f32[128,512]{1,0:T(8,128)S(1)}, f32[128,512]{1,0:T(8,128)}, u32[]{:S(2)}) copy-start(f32[128,512]{1,0:T(8,128)} %param.29) | copy-start | bytes 786436
  117.3 86.6 %all-gather.24.cloned.1.call-start = ((), (), s32[]{:S(2)}) async-start(), calls=%async_computation.7 | async-start | bytes 1310720 | tf_op jit(solution)/shard_map/while/body/eval_jaxpr/all_gather | solution.py:126
  180.2 101.7 %copy-start.10 = (bf16[4096]{0:T(1024)(128)(2,1)S(1)}, bf16[4096]{0:T(1024)(128)(2,1)}, u32[]{:S(2)}) copy-start(bf16[4096]{0:T(1024)(128)(2,1)} %param.24) | copy-start | bytes 24580
  181.0 49.1 %all-gather.28.cloned.1.call-start = ((), (), s32[]{:S(2)}) async-start(), calls=%async_computation.9 | async-start | bytes 1310720 | tf_op jit(solution)/shard_map/while/body/eval_jaxpr/all_gather | solution.py:174
  181.0 4.9 collective-permute-start
  186.0 105.3 %copy-start.11 = (f32[128]{0:T(128)S(1)}, f32[128]{0:T(128)}, u32[]{:S(2)}) copy-start(f32[128]{0:T(128)} %param.31) | copy-start | bytes 1540
  186.1 96.5 %copy-start.1 = (f32[2,128,512]{2,1,0:T(8,128)}, f32[2,128,512]{2,1,0:T(8,128)S(1)}, u32[]{:S(2)}) copy-start(f32[2,128,512]{2,1,0:T(8,128)S(1)} %broadcast_multiply_fusion) | copy-start | bytes 1572868
  186.9 69.1 %all-gather.20.cloned.1.call-start = ((), (), s32[]{:S(2)}) async-start(), calls=%async_computation.5 | async-start | bytes 1310720 | tf_op jit(solution)/shard_map/all_gather | solution.py:134
  206.6 75.3 %all-gather.22.cloned.1.call-start = ((), (), s32[]{:S(2)}) async-start(), calls=%async_computation.6 | async-start | bytes 1310720 | tf_op jit(solution)/shard_map/all_gather | solution.py:182
  232.7 120.8 %copy-start.5 = (f32[128,512]{1,0:T(8,128)S(1)}, f32[128,512]{1,0:T(8,128)}, u32[]{:S(2)}) copy-start(f32[128,512]{1,0:T(8,128)} %fusion.28) | copy-start | bytes 786436
  232.7 167.3 %all-gather.26.cloned.1.call-start = ((), (), s32[]{:S(2)}) async-start(), calls=%async_computation.8 | async-start | bytes 34603008 | tf_op jit(solution)/shard_map/all_gather | solution.py:9
  256.0 376.1 %all-gather.30.cloned.1.call-start = ((), (), s32[]{:S(2)}) async-start(), calls=%async_computation.10 | async-start | bytes 34603008 | tf_op jit(solution)/shard_map/all_gather | solution.py:9
  282.5 15.6 %all-to-all-start.3 = ((bf16[32,128,1]{1,2,0:T(2,128)(2,1)}), bf16[32,128,1]{1,2,0:T(2,128)(2,1)S(1)}, u32[]{:S(2)}, u32[]{:S(2)}) async-start(bf16[32,128,1]{1,2,0:T(2,128)(2,1)} %copy.30), calls=%async_computation.3 | async-start | bytes 32768 | tf_op jit(solution)/shard_map/all_to_all | solution.py:94
  353.6 46.5 %copy-start.3 = (f32[2,128,512]{2,1,0:T(8,128)}, f32[2,128,512]{2,1,0:T(8,128)S(1)}, u32[]{:S(2)}) copy-start(f32[2,128,512]{2,1,0:T(8,128)S(1)} %bitcast_dynamic-update-slice_fusion.1) | copy-start | bytes 1572868
  400.1 231.2 %copy-start.4 = (f32[128,512]{1,0:T(8,128)S(1)}, f32[128,512]{1,0:T(8,128)}, u32[]{:S(2)}) copy-start(f32[128,512]{1,0:T(8,128)} %fusion.26) | copy-start | bytes 786436
  577.8 128.0 %copy-start.9 = (f32[2,128]{1,0:T(2,128)}, f32[2,128]{1,0:T(2,128)S(1)}, u32[]{:S(2)}) copy-start(f32[2,128]{1,0:T(2,128)S(1)} %add.145) | copy-start | bytes 3076
  632.1 73.3 %copy-start.2 = (f32[2,128,512]{2,1,0:T(8,128)S(1)}, f32[2,128,512]{2,1,0:T(8,128)}, u32[]{:S(2)}) copy-start(f32[2,128,512]{2,1,0:T(8,128)} %bitcast_dynamic-update-slice_fusion) | copy-start | bytes 1572868
Sparse Core Ops, SparseCore 0:
  117.5 58.2 all-reduce.1
  181.1 22.8 all-gather.23
  205.7 24.2 all-gather.27
  231.7 24.2 all-gather.19
  257.6 24.2 all-gather.21
  284.3 115.7 all-gather.25
  402.6 113.1 all-gather.29
where the time goes:
time: 718 us; the launch traced here: 713 us
  matrix products  273 us (38%)
  waiting for transfers between devices  252 us (35%)
  blocking collectives  118 us (16%)
  starting transfers between devices  26.2 us (4%)
  local copies, waits for them, and re-layouts  17.7 us (2%)
  between operations  14.5 us (2%)
  other arithmetic  8.56 us (1%)
    dot_general x64, matrix products, compose(): jnp.dot(subsequent_dates[0], earlier[1], precision=maximal_accuracy)  142 us
    dot_general x32, matrix products, compose(): jnp.dot(subsequent_dates[0], earlier[0], precision=maximal_accuracy)  98.4 us
    all_gather x2, blocking collectives, carried_in(): everything = jax.tree.map(lambda part: lax.all_gather(part, axis), x)  59.8 us
    psum x1, waiting for transfers between devices, local(): omega, info = lax.psum((omega_part, info_part), 'obs')  58.3 us
    all_to_all x1, waiting for transfers between devices, local(): lax.all_to_all(records, 'tm', split_axis=0, concat_axis=0, tiled=True)  48.9 us
    all_gather x2, waiting for transfers between devices, carried_in(): everything = jax.tree.map(lambda part: lax.all_gather(part, axis), x)  46.5 us
    all_gather x1, waiting for transfers between devices, local(): lax.all_gather(chains[0], 'obs', axis=0, tiled=True)  25.8 us
    all_gather x1, waiting for transfers between devices, backward_day(): lax.all_gather(previous[0], 'obs', axis=0, tiled=True)  23.4 us
  transfers between devices with their start and end apart: 11, of which 10 were waited for; matrix products, arithmetic and copies ran while one was open for 27% of the time, Pallas kernels for 0%

commit v1 on v0

v1 whole, which is shorter than its diff:
```python
import jax
import jax.numpy as jnp
from jax import lax
from jax.experimental import pallas as pl
from jax.experimental.pallas import tpu as pltpu
from jax.sharding import PartitionSpec as P

MESH = pl.DeviceIdType.MESH
F32 = jnp.float32
BF16 = jnp.bfloat16
HIGH = lax.Precision.HIGHEST
S = 512


def row_place(r):
    g, i = r // 4, r % 4
    im = i % 3
    return (2 * (g % 2) + im * (im + 1) // 2) % 4, (g + i // 3) % 4


def place_row(y, z):
    phi = (y + 2 * z) % 4
    i = phi + (phi // 2) * (5 - 2 * phi)
    g = (z - i // 3 + 4) % 4
    return g, i


def row_times(ref, row):
    parts = []
    for k in range(0, S, 128):
        block = ref[k:k + 128, :]
        total = block[:, 0:128] * row[:, 0:128]
        for n in range(128, S, 128):
            total = total + block[:, n:n + 128] * row[:, n:n + 128]
        parts.append(jnp.sum(total, axis=1, keepdims=True))
    return jnp.concatenate(parts, axis=0)


def col_times(ref, col):
    total = ref[0:32, :] * col[0:32, :]
    for k in range(32, S, 32):
        total = total + ref[k:k + 32, :] * col[k:k + 32, :]
    return jnp.sum(total, axis=0, keepdims=True)


def to_row(col):
    return jnp.broadcast_to(col, (S, 128)).T[0:1, :]


def dot(a, b):
    return jnp.dot(a, b, precision=HIGH, preferred_element_type=F32)


def dot_nt(a, b):
    return lax.dot_general(a, b, (((1,), (1,)), ((), ())), precision=HIGH, preferred_element_type=F32)


def kernel(rec, meta, prop, cov, kslab, damp, prior, filt_out, smooth_out,
           land, mland, lhs, acc, r1, hs, r2, fh, r3, ri, om, wide, slab, slab_t, brow, maps, brows, kfull, k_t,
           dsrc, dl, psrc, pr, hop_src, hop_in, start_src, start_in, msg, mail,
           s_rec, r_rec, s_meta, r_meta, s_k, r_k, s_d, r_d, s_p, r_p, s_1, r_1, s_i, r_i, s_2, r_2, s_3, r_3,
           s_a, r_a, s_b, r_b, s_h, r_h, s_s, r_s, s_m, r_m, l_rec, l_meta):
    tm, x = lax.axis_index("tm"), lax.axis_index("obs")
    z, y, core = tm // 8, (tm // 2) % 4, tm % 2
    q, xi = x // 2, x % 2
    g, i_row = place_row(y, z)
    e_me = 2 * i_row + q
    c_me = 8 * g + e_me
    j = 2 * xi + core
    lead_tm = g * 8 + (2 * (g % 2)) * 2
    is_lead = jnp.logical_and(tm == lead_tm, x == 1)
    sib = tm + 1 - 2 * core
    xp = x + 1 - 2 * xi

    def remote(src, dst, ss, rs, dev):
        return pltpu.make_async_remote_copy(src_ref=src, dst_ref=dst, send_sem=ss, recv_sem=rs, device_id=dev,
                                            device_id_type=MESH)

    me = tm * 4 + x
    barrier = pltpu.get_barrier_semaphore()

    def greet(n, carry):
        other = (me + n) % 128
        pl.semaphore_signal(barrier, 1, device_id=(other // 4, other % 4), device_id_type=MESH)
        return carry

    lax.fori_loop(1, 128, greet, 0)
    pl.semaphore_wait(barrier, 127)

    def offset(m):
        return 1 + ((m - 1) * 11 + core * 15) % 31

    def record_copies(m):
        o = offset(m)
        dq, ty, tz = o // 16, (y + (o // 4) % 4) % 4, (z + o % 4) % 4
        tq = (q + dq) % 2
        tx = x + dq * (3 - 2 * x)
        tg, ti = place_row(ty, tz)
        c = 8 * tg + 2 * ti + tq
        dev = (tz * 8 + ty * 2 + core, tx)
        return (
            remote(rec.at[pl.ds(pl.multiple_of(c * 128, 128), 128)],
                   land.at[m // 2, pl.ds(pl.multiple_of((m % 2) * 128, 128), 128)], s_rec.at[m], r_rec.at[m], dev),
            remote(meta.at[c], mland.at[m], s_meta.at[m], r_meta.at[m], dev),
        )

    own_rec = pltpu.make_async_copy(rec.at[pl.ds(pl.multiple_of(c_me * 128, 128), 128)],
                                    land.at[0, pl.ds(0, 128)], l_rec)
    own_rec.start()
    own_meta = pltpu.make_async_copy(meta.at[c_me], mland.at[0], l_meta)
    own_meta.start()

    def send_record(m, carry):
        a, b = record_copies(m)
        b.start()
        a.start()
        return carry

    dsrc[...] = jnp.zeros_like(dsrc)
    dsrc[0:2, :] = damp[...]
    dr_y, dr_z = row_place(tm // 2)
    d_tm, d_x = dr_z * 8 + dr_y * 2 + x % 2, 2 * (tm % 2) + x // 2
    d_self = jnp.logical_and(d_tm == tm, d_x == x)
    d_copy = remote(dsrc, dl, s_d.at[0], r_d.at[0], (d_tm, d_x))

    @pl.when(d_self)
    def _():
        dl[...] = dsrc[...]

    @pl.when(jnp.logical_not(d_self))
    def _():
        d_copy.start()

    psrc[...] = jnp.broadcast_to(prior[...], (8, 128))
    p_copy = remote(psrc, pr.at[x], s_p.at[0], r_p.at[x], (0, 1))
    p_send = jnp.logical_and(tm == 0, x != 1)

    @pl.when(p_send)
    def _():
        p_copy.start()

    @pl.when(jnp.logical_and(tm == 0, x == 1))
    def _():
        pr[1] = psrc[...]

    lax.fori_loop(1, 32, send_record, 0)

    def gain_copy(n):
        return remote(kslab, kfull.at[pl.ds(pl.multiple_of(x * 128, 128), 128)], s_k.at[n], r_k.at[n],
                      (tm, (x + n) % 4))

    def gain_in(n):
        ox = (x - n + 4) % 4
        return remote(kslab, kfull.at[pl.ds(pl.multiple_of(ox * 128, 128), 128)], s_k.at[n], r_k.at[n], (tm, xp))

    for n in range(1, 4):
        gain_copy(n).start()
    kfull[pl.ds(pl.multiple_of(x * 128, 128), 128), :] = kslab[...]

    acc[...] = jnp.zeros_like(acc)
    own_rec.wait()
    own_meta.wait()

    def wait_record(m):
        a, b = record_copies(m)
        b.wait_recv()
        a.wait_recv()

    def gram(p, carry):
        @pl.when(p > 0)
        def _():
            wait_record(2 * p)
        wait_record(2 * p + 1)
        rows = land[p]
        marks = jnp.concatenate([mland[2 * p], mland[2 * p + 1]], axis=1)
        rows_t = rows.T
        lhs[0:512, :] = rows_t * marks[2:3, :]
        lhs[512:1024, :] = rows_t * marks[3:4, :]
        lhs[1024:1040, :] = marks
        acc[...] += jnp.dot(lhs[...], rows, preferred_element_type=F32)
        return carry

    lax.fori_loop(0, 16, gram, 0)

    for n in range(1, 4):
        gain_in(n).wait_recv()
    k_t[...] = kfull[...].T

    mine, theirs = pl.multiple_of(128 * core, 128), pl.multiple_of(128 * (1 - core), 128)

    def first_copies(d):
        return (
            remote(acc.at[pl.ds(d * 512 + theirs, 128), :], r1.at[d, :, pl.ds(0, 512)], s_1.at[2 * d], r_1.at[2 * d],
                   (sib, x)),
            remote(acc.at[pl.ds(d * 512 + 256 + theirs, 128), pl.ds(256, 256)], r1.at[d, :, pl.ds(512, 256)],
                   s_1.at[2 * d + 1], r_1.at[2 * d + 1], (sib, x)),
        )

    peers = ((sib, x), (tm, xp), (sib, xp))
    info_copies = [remote(acc.at[pl.ds(1024, 8), :], ri.at[n], s_i.at[n], r_i.at[n], peers[n]) for n in range(3)]
    for d in range(2):
        for copy in first_copies(d):
            copy.start()
    for copy in info_copies:
        copy.start()
    second = [remote(hs.at[d], r2.at[d], s_2.at[d], r_2.at[d], (tm, xp)) for d in range(2)]
    third = [remote(fh.at[d], r3.at[d], s_3.at[d], r_3.at[d], (sib, x)) for d in range(2)]
    for d in range(2):
        for copy in first_copies(d):
            copy.wait_recv()
        hs[d, :, 0:512] = acc[pl.ds(d * 512 + mine, 128), :] + r1[d, :, 0:512]
        hs[d, :, 512:768] = acc[pl.ds(d * 512 + 256 + mine, 128), 256:512] + r1[d, :, 512:768]
        second[d].start()
    for copy in info_copies:
        copy.wait_recv()
    info = (acc[1024:1032, :] + ri[0]) + (ri[1] + ri[2])

    @pl.when(jnp.logical_not(d_self))
    def _():
        d_copy.wait_recv()

    d_rows = dl[...]
    d_cols = d_rows.T

    wide[0:128, :] = prop[:, pl.ds(pl.multiple_of(j * 128, 128), 128)].T * d_rows[0:1, :]
    wide[128:136, :] = jnp.zeros((8, S), F32)
    for d in range(2):
        second[d].wait_recv()
        fh[d] = hs[d] + r2[d]
        third[d].start()
        om[d, pl.ds(mine, 128), :] = fh[d, :, 0:512]
        om[d, pl.ds(256 + mine, 128), 256:512] = fh[d, :, 512:768]
        third[d].wait_recv()
        om[d, pl.ds(theirs, 128), :] = r3[d, :, 0:512]
        om[d, pl.ds(256 + theirs, 128), 256:512] = r3[d, :, 512:768]
        om[d, 256:512, 0:256] = om[d, 0:256, 256:512].T
        if d == 1:
            wide[...] = dot_nt(wide[...], prop[...]) * d_rows[1:2, :]
        w = wide[...]
        seen = jnp.concatenate([jnp.zeros((128, S), F32), jnp.broadcast_to(info[d:d + 1, :], (8, S))], axis=0)
        wide[...] = w - dot(dot(w, om[d]) - seen, cov[...])

    lead = (lead_tm, 1)
    slab_cols = pl.multiple_of(j * 128, 128)
    even_copy = remote(slab_t, maps.at[e_me, :, pl.ds(slab_cols, 128)], s_a.at[0], r_a.at[e_me * 4 + j], lead)
    odd_copy = remote(slab, maps.at[e_me, pl.ds(slab_cols, 128), :], s_a.at[0], r_a.at[e_me * 4 + j], lead)
    b_copy = remote(brow, brows.at[e_me], s_b.at[0], r_b.at[e_me], lead)

    @pl.when(q == 0)
    def _():
        slab_t[...] = wide[0:128, :].T

    @pl.when(q == 1)
    def _():
        slab[...] = wide[0:128, :]

    @pl.when(is_lead)
    def _():
        maps[0, :, 256:384] = slab_t[...]

    even_send = jnp.logical_and(q == 0, jnp.logical_not(is_lead))

    @pl.when(even_send)
    def _():
        even_copy.start()

    @pl.when(q == 1)
    def _():
        odd_copy.start()

    brow[...] = wide[128:136, :]

    @pl.when(j == 0)
    def _():
        b_copy.start()

    next_g = (g + 1) % 4
    hop_copy = remote(hop_src, hop_in, s_h.at[0], r_h.at[0], (next_g * 8 + (2 * (next_g % 2)) * 2, 1))

    def start_copy(e, n):
        sy, sz = row_place(4 * g + e // 2)
        return remote(start_src.at[e], start_in, s_s.at[e * 4 + n], r_s.at[0],
                      (sz * 8 + sy * 2 + n % 2, 2 * (e % 2) + n // 2))

    @pl.when(is_lead)
    def _():
        @pl.when(g == 0)
        def _():
            for ox in (0, 2, 3):
                remote(psrc, pr.at[ox], s_p.at[0], r_p.at[ox], (0, 0)).wait_recv()
            for ox in range(4):
                hop_in[:, 128 * ox:128 * ox + 128] = pr[ox]

        for e in range(8):
            for n in range(4):
                if (e, n) == (0, 2):
                    continue
                if e % 2 == 0:
                    remote(slab_t, maps.at[e, :, pl.ds(128 * n, 128)], s_a.at[0], r_a.at[e * 4 + n],
                           (sib, x)).wait_recv()
                else:
                    remote(slab, maps.at[e, pl.ds(128 * n, 128), :], s_a.at[0], r_a.at[e * 4 + n],
                           (sib, x)).wait_recv()
            remote(brow, brows.at[e], s_b.at[0], r_b.at[e], (sib, x)).wait_recv()

        @pl.when(g > 0)
        def _():
            hop_copy.wait_recv()

        row = hop_in[0:1, :]
        for e in range(0, 8, 2):
            start_src[e] = jnp.broadcast_to(row, (8, S))
            for n in range(4):
                if (e, n) != (0, 2):
                    start_copy(e, n).start()
            if e == 0:
                start_in[...] = start_src[0]
            col = row_times(maps.at[e], row) + brows[e].T[:, 0:1]
            row = col_times(maps.at[e + 1], col) + brows[e + 1, 0:1, :]
            if e == 6:
                hop_src[...] = jnp.broadcast_to(row, (8, S))

                @pl.when(g < 3)
                def _():
                    hop_copy.start()
            start_src[e + 1] = jnp.broadcast_to(to_row(col), (8, S))
            for n in range(4):
                start_copy(e + 1, n).start()

    @pl.when(jnp.logical_not(is_lead))
    def _():
        start_copy(0, 0).wait_recv()

    before = start_in[0:1, :]
    moved = d_cols[:, 0:1] * row_times(prop, before)
    first_col = moved - row_times(cov, col_times(om.at[0], moved) - info[0:1, :])
    first = to_row(first_col)
    ahead_col = row_times(prop, first)
    moved = d_cols[:, 1:2] * ahead_col
    second_col = moved - row_times(cov, col_times(om.at[1], moved) - info[1:2, :])
    last = to_row(second_col)
    msg[0:1, :] = first
    msg[1:2, :] = last
    msg[2:3, :] = to_row(ahead_col)
    msg[3:4, :] = to_row(row_times(prop, last))
    msg[4:6, :] = d_rows[0:2, :]
    msg[6:8, :] = jnp.zeros((2, S), F32)

    def mail_copy(n):
        return remote(msg, mail.at[c_me], s_m.at[n], r_m.at[c_me], ((tm + n) % 32, j))

    to_self = j == x

    @pl.when(to_self)
    def _():
        mail[c_me] = msg[...]

    @pl.when(jnp.logical_not(to_self))
    def _():
        mail_copy(0).start()

    def post(n, carry):
        mail_copy(n).start()
        return carry

    lax.fori_loop(1, 32, post, 0)

    def wait_mail(c):
        @pl.when(jnp.logical_not(jnp.logical_and(to_self, c == c_me)))
        def _():
            remote(msg, mail.at[c], s_m.at[0], r_m.at[c], (sib, x)).wait_recv()

    own_cols = pl.ds(pl.multiple_of(x * 128, 128), 128)

    def back(n, carry):
        state, damp_next = carry
        c = 31 - n
        wait_mail(c)
        rows = mail[c]
        cols = rows.T
        gap = damp_next * (state - damp_next * rows[3:4, :])
        later = cols[:, 1:2] + row_times(kfull, gap)
        gap_col = cols[:, 5:6] * (later - cols[:, 5:6] * cols[:, 2:3])
        state = rows[0:1, :] + col_times(k_t, gap_col)

        @pl.when(c == tm)
        def _():
            hs[0, 0:1, 0:512] = state
            hs[0, 8:9, 0:512] = to_row(later)

        return state, rows[4:5, :]

    for d in range(2):
        second[d].wait_send()
    zero = jnp.zeros((1, S), F32)
    lax.fori_loop(0, 32 - tm, back, (zero, zero))
    smooth_out[0:1, :] = hs[0, 0:1, own_cols]
    smooth_out[1:2, :] = hs[0, 8:9, own_cols]
    filt_out[...] = mail[tm, 0:2, own_cols]

    def drain_mail(n, carry):
        wait_mail(n)
        return carry

    lax.fori_loop(0, tm, drain_mail, 0)

    def drain_record(m, carry):
        a, b = record_copies(m)
        a.wait_send()
        b.wait_send()
        return carry

    lax.fori_loop(1, 32, drain_record, 0)

    def drain_post(n, carry):
        mail_copy(n).wait_send()
        return carry

    lax.fori_loop(1, 32, drain_post, 0)

    @pl.when(jnp.logical_not(to_self))
    def _():
        mail_copy(0).wait_send()

    for n in range(1, 4):
        gain_copy(n).wait_send()

    @pl.when(jnp.logical_not(d_self))
    def _():
        d_copy.wait_send()

    @pl.when(p_send)
    def _():
        p_copy.wait_send()

    for d in range(2):
        for copy in first_copies(d):
            copy.wait_send()
        third[d].wait_send()
    for copy in info_copies:
        copy.wait_send()

    @pl.when(even_send)
    def _():
        even_copy.wait_send()

    @pl.when(q == 1)
    def _():
        odd_copy.wait_send()

    @pl.when(j == 0)
    def _():
        b_copy.wait_send()

    @pl.when(is_lead)
    def _():
        for e in range(8):
            for n in range(4):
                if (e, n) != (0, 2):
                    start_copy(e, n).wait_send()

        @pl.when(g < 3)
        def _():
            hop_copy.wait_send()


def local(records, obs_values, block_day, block_count, propagator_matrix, analysis_cov, unattenuated_multiplier,
          damping, prior_mean):
    slot = lax.broadcasted_iota(jnp.int32, (32, 16, 128), 2)
    part = lax.broadcasted_iota(jnp.int32, (32, 16, 128), 1)
    held = jnp.logical_and(slot < block_count[:, None, None], block_day[:, None, None] == part % 2)
    held = jnp.logical_and(held, part < 4)
    values = jnp.where(part < 2, obs_values.reshape(32, 1, 128), jnp.ones((), BF16))
    meta = jnp.where(held, values, jnp.zeros((), BF16))
    vmem = pl.BlockSpec(memory_space=pltpu.VMEM)
    dma = pltpu.SemaphoreType.DMA
    return pl.pallas_call(
        kernel,
        out_shape=(jax.ShapeDtypeStruct((2, 128), F32), jax.ShapeDtypeStruct((2, 128), F32)),
        in_specs=[pl.BlockSpec(memory_space=pl.ANY)] + [vmem] * 6,
        out_specs=(vmem, vmem),
        scratch_shapes=[
            pltpu.VMEM((16, 256, S), BF16),
            pltpu.VMEM((32, 16, 128), BF16),
            pltpu.VMEM((1040, 256), BF16),
            pltpu.VMEM((1040, S), F32),
            pltpu.VMEM((2, 128, 768), F32),
            pltpu.VMEM((2, 128, 768), F32),
            pltpu.VMEM((2, 128, 768), F32),
            pltpu.VMEM((2, 128, 768), F32),
            pltpu.VMEM((2, 128, 768), F32),
            pltpu.VMEM((3, 8, S), F32),
            pltpu.VMEM((2, S, S), F32),
            pltpu.VMEM((136, S), F32),
            pltpu.VMEM((128, S), F32),
            pltpu.VMEM((S, 128), F32),
            pltpu.VMEM((8, S), F32),
            pltpu.VMEM((8, S, S), F32),
            pltpu.VMEM((8, 8, S), F32),
            pltpu.VMEM((S, S), F32),
            pltpu.VMEM((S, S), F32),
            pltpu.VMEM((8, S), F32),
            pltpu.VMEM((8, S), F32),
            pltpu.VMEM((8, 128), F32),
            pltpu.VMEM((4, 8, 128), F32),
            pltpu.VMEM((8, S), F32),
            pltpu.VMEM((8, S), F32),
            pltpu.VMEM((8, 8, S), F32),
            pltpu.VMEM((8, S), F32),
            pltpu.VMEM((8, S), F32),
            pltpu.VMEM((32, 8, S), F32),
            dma((32,)), dma((32,)), dma((32,)), dma((32,)),
            dma((4,)), dma((4,)), dma((1,)), dma((1,)), dma((1,)), dma((4,)),
            dma((4,)), dma((4,)), dma((3,)), dma((3,)), dma((2,)), dma((2,)), dma((2,)), dma((2,)),
            dma((1,)), dma((32,)), dma((1,)), dma((8,)), dma((1,)), dma((1,)),
            dma((32,)), dma((1,)), dma((32,)), dma((32,)), dma, dma,
        ],
        compiler_params=pltpu.CompilerParams(collective_id=0, has_side_effects=True, vmem_limit_bytes=56 << 20),
        cost_estimate=pl.CostEstimate(flops=10**10, bytes_accessed=10**8, transcendentals=0),
    )(records, meta, propagator_matrix, analysis_cov, unattenuated_multiplier, damping, prior_mean.reshape(1, 128))


def solution(mesh):
    return jax.shard_map(
        local,
        mesh=mesh,
        in_specs=(
            P(("tm", "obs"), None),
            P(("tm", "obs")),
            P(("tm", "obs")),
            P(("tm", "obs")),
            P(),
            P(),
            P("obs", None),
            P("tm", None),
            P("obs"),
        ),
        out_specs=(P("tm", "obs"), P("tm", "obs")),
        check_vma=False,
    )
```

time: 718 us -> 184 us (0.26)
  matrix products: 273 us -> 0 us
  waiting for transfers between devices: 252 us -> 0 us
  Pallas kernels: 0 us -> 179 us
  blocking collectives: 118 us -> 0 us
  starting transfers between devices: 26.2 us -> 0 us
  local copies, waits for them, and re-layouts: 17.7 us -> 2.43 us
  between operations: 14.5 us -> 0.66 us
    dot_general x112 -> x0, matrix products: 273 us -> none  [the longest x64 142 us: compose(): jnp.dot(subsequent_dates[0], earlier[1], precision=maximal_accuracy)]
    pallas_call x0 -> x1, Pallas kernels: none -> 179 us  [local(): pl.pallas_call(kernel, out_shape=(jax.ShapeDtypeStruct((2, 128), F32), ja...]
    all_gather x6 -> x0, waiting for transfers between devices: 136 us -> none  [the longest x2 46.5 us: carried_in(): everything = jax.tree.map(lambda part: lax.all_gather(part, axis), x)]
    all_gather x8 -> x0, blocking collectives: 98.7 us -> none  [the longest x2 59.8 us: carried_in(): everything = jax.tree.map(lambda part: lax.all_gather(part, axis), x)]
    psum x1 -> x0, waiting for transfers between devices: 58.3 us -> none  [local(): omega, info = lax.psum((omega_part, info_part), 'obs')]
    all_to_all x3 -> x0, waiting for transfers between devices: 55.2 us -> none  [the longest x1 48.9 us: local(): lax.all_to_all(records, 'tm', split_axis=0, concat_axis=0, tiled=True)]
    all_to_all x3 -> x0, starting transfers between devices: 23.3 us -> none  [the longest x1 9.6 us: local(): lax.all_to_all(block_day, 'tm', split_axis=0, concat_axis=0, tiled=True)]
    all_to_all x1 -> x0, blocking collectives: 10.7 us -> none  [local(): lax.all_to_all(block_count, 'tm', split_axis=0, concat_axis=0, tiled=True)]
  transfers between devices with their start and end apart: 11 -> 0, of which waited for: 10 -> 0; matrix products, arithmetic and copies ran while one was open for 27% -> 0% of each run, Pallas kernels for 0% -> 0%
where the time goes in v1:
time: 184 us
  Pallas kernels  179 us (97%)
  local copies, waits for them, and re-layouts  2.43 us (1%)
    pallas_call x1, Pallas kernels, local(): pl.pallas_call(kernel, out_shape=(jax.ShapeDtypeStruct((2, 128), F32), ja...  179 us

profile of v1, /device:TPU:1, one launch (start us, length us, event | category | flops | bytes accessed | tf_op | source)
XLA Modules:
  0.0 183.5 jit_solution(6487506482563933588)
XLA Ops:
  0.7 1.6 fusion.2.meta
  2.2 178.9 %shard_map.104 = (f32[2,128]{1,0:T(2,128)}, f32[2,128]{1,0:T(2,128)}) custom-call(bf16[4096,512]{1,0:T(8,128)(2,1)} %rec.1, bf16[32,16,128]{2,1,0:T(8,128)(2,1)} %fusion.2.meta, f32[512,512]{1,0:T(8,128)} %prop.1, f32[512,512]{1,0:T(8,128)} %cov.1, f32[128,512]{1,0:T(8,128)} %kslab.1, f32[2,512]{1,0:T(2,128)} %damp.1, f32[1,128]{1,0:T(1,128)} %bitcast.3), custom_call_target="tpu_custom_call" | custom-call | flops 10000000000 | bytes 100000000 | tf_op jit(solution)/shard_map/pallas_call | solution.py:477
  181.1 1.2 copy.13
  182.3 1.2 copy.14
  (3 shorter events, 0.0 us)

commit v2 on v1

--- a/solution.py
+++ b/solution.py
@@ -26,25 +26,59 @@
 
 
 def row_times(ref, row):
-    parts = []
-    for k in range(0, S, 128):
-        block = ref[k:k + 128, :]
-        total = block[:, 0:128] * row[:, 0:128]
-        for n in range(128, S, 128):
-            total = total + block[:, n:n + 128] * row[:, n:n + 128]
-        parts.append(jnp.sum(total, axis=1, keepdims=True))
-    return jnp.concatenate(parts, axis=0)
-
-
-def col_times(ref, col):
-    total = ref[0:32, :] * col[0:32, :]
-    for k in range(32, S, 32):
-        total = total + ref[k:k + 32, :] * col[k:k + 32, :]
-    return jnp.sum(total, axis=0, keepdims=True)
-
-
-def to_row(col):
-    return jnp.broadcast_to(col, (S, 128)).T[0:1, :]
+    wide = jnp.broadcast_to(row, (8, S))
+    tiles = []
+    for k in range(0, S, 8):
+        t = [ref[k:k + 8, n:n + 128] * wide[:, n:n + 128] for n in range(0, S, 128)]
+        tiles.append(jnp.broadcast_to(jnp.sum((t[0] + t[1]) + (t[2] + t[3]), axis=1, keepdims=True), (8, 128)))
+    return tiles
+
+
+def col_times(ref, tiles):
+    out = []
+    for n in range(0, S, 128):
+        total = [None] * 4
+        for k in range(64):
+            p = ref[8 * k:8 * k + 8, n:n + 128] * tiles[k]
+            total[k % 4] = p if total[k % 4] is None else total[k % 4] + p
+        out.append(jnp.sum((total[0] + total[1]) + (total[2] + total[3]), axis=0, keepdims=True))
+    return jnp.concatenate(out, axis=1)
+
+
+def diagonals():
+    lead = lax.broadcasted_iota(jnp.int32, (8, 128), 1) - lax.broadcasted_iota(jnp.int32, (8, 128), 0)
+    return [lead == 8 * k for k in range(16)]
+
+
+def to_row(tiles):
+    marks = diagonals()
+    out = []
+    for n in range(4):
+        picked = [jnp.where(marks[k], tiles[16 * n + k], 0.0) for k in range(16)]
+        while len(picked) > 1:
+            picked = [picked[k] + picked[k + 1] for k in range(0, len(picked), 2)]
+        out.append(jnp.sum(picked[0], axis=0, keepdims=True))
+    return jnp.concatenate(out, axis=1)
+
+
+def to_tiles(row):
+    marks = diagonals()
+    tiles = []
+    for n in range(4):
+        part = jnp.broadcast_to(row[:, 128 * n:128 * n + 128], (8, 128))
+        for k in range(16):
+            tiles.append(jnp.broadcast_to(
+                jnp.sum(jnp.where(marks[k], part, 0.0), axis=1, keepdims=True), (8, 128)))
+    return tiles
+
+
+def keep(ref, tiles):
+    for k in range(64):
+        ref[8 * k:8 * k + 8, :] = tiles[k]
+
+
+def kept_tile(ref, k):
+    return ref[8 * k:8 * k + 8, :]
 
 
 def dot(a, b):
@@ -57,7 +91,7 @@
 
 def kernel(rec, meta, prop, cov, kslab, damp, prior, filt_out, smooth_out,
            land, mland, lhs, acc, r1, hs, r2, fh, r3, ri, om, wide, slab, slab_t, brow, maps, brows, kfull, k_t,
-           dsrc, dl, psrc, pr, hop_src, hop_in, start_src, start_in, msg, mail,
+           dsrc, dl, psrc, pr, hop_src, hop_in, start_src, start_in, msg, mail, kept, mail_tiles, d_tiles, b_tiles,
            s_rec, r_rec, s_meta, r_meta, s_k, r_k, s_d, r_d, s_p, r_p, s_1, r_1, s_i, r_i, s_2, r_2, s_3, r_3,
            s_a, r_a, s_b, r_b, s_h, r_h, s_s, r_s, s_m, r_m, l_rec, l_meta):
     tm, x = lax.axis_index("tm"), lax.axis_index("obs")
@@ -76,25 +110,44 @@
         return pltpu.make_async_remote_copy(src_ref=src, dst_ref=dst, send_sem=ss, recv_sem=rs, device_id=dev,
                                             device_id_type=MESH)
 
-    me = tm * 4 + x
+    drains = []
+
+    def sent(copy, when=None):
+        if when is None:
+            drains.append(copy.wait_send)
+        else:
+            drains.append(lambda: pl.when(when)(copy.wait_send))
+
     barrier = pltpu.get_barrier_semaphore()
 
-    def greet(n, carry):
-        other = (me + n) % 128
-        pl.semaphore_signal(barrier, 1, device_id=(other // 4, other % 4), device_id_type=MESH)
-        return carry
-
-    lax.fori_loop(1, 128, greet, 0)
-    pl.semaphore_wait(barrier, 127)
+    def owner_of(o):
+        dq, dy, dz = o // 16, (o // 4) % 4, o % 4
+        return ((z + dz) % 4, (y + dy) % 4, (q + dq) % 2, x + dq * (3 - 2 * x)), (
+            ((z - dz + 4) % 4) * 8 + ((y - dy + 4) % 4) * 2 + core, x + dq * (3 - 2 * x))
+
+    dr_y, dr_z = row_place(tm // 2)
+    d_tm, d_x = dr_z * 8 + dr_y * 2 + x % 2, 2 * (tm % 2) + x // 2
+    d_self = jnp.logical_and(d_tm == tm, d_x == x)
+
+    def greet(dev):
+        pl.semaphore_signal(barrier, 1, device_id=dev, device_id_type=MESH)
+
+    def greet_source(o, carry):
+        greet(owner_of(o)[1])
+        return carry
+
+    lax.fori_loop(1, 32, greet_source, 0)
+    for dev in ((tm, (x + 1) % 4), (tm, (x + 2) % 4), (tm, (x + 3) % 4), (sib, x), (sib, xp),
+                (c_me, 2 * xi + core)):
+        greet(dev)
+    pl.semaphore_wait(barrier, 37)
 
     def offset(m):
         return 1 + ((m - 1) * 11 + core * 15) % 31
 
     def record_copies(m):
         o = offset(m)
-        dq, ty, tz = o // 16, (y + (o // 4) % 4) % 4, (z + o % 4) % 4
-        tq = (q + dq) % 2
-        tx = x + dq * (3 - 2 * x)
+        tz, ty, tq, tx = owner_of(o)[0]
         tg, ti = place_row(ty, tz)
         c = 8 * tg + 2 * ti + tq
         dev = (tz * 8 + ty * 2 + core, tx)
@@ -118,9 +171,6 @@
 
     dsrc[...] = jnp.zeros_like(dsrc)
     dsrc[0:2, :] = damp[...]
-    dr_y, dr_z = row_place(tm // 2)
-    d_tm, d_x = dr_z * 8 + dr_y * 2 + x % 2, 2 * (tm % 2) + x // 2
-    d_self = jnp.logical_and(d_tm == tm, d_x == x)
     d_copy = remote(dsrc, dl, s_d.at[0], r_d.at[0], (d_tm, d_x))
 
     @pl.when(d_self)
@@ -130,6 +180,8 @@
     @pl.when(jnp.logical_not(d_self))
     def _():
         d_copy.start()
+
+    sent(d_copy, jnp.logical_not(d_self))
 
     psrc[...] = jnp.broadcast_to(prior[...], (8, 128))
     p_copy = remote(psrc, pr.at[x], s_p.at[0], r_p.at[x], (0, 1))
@@ -139,11 +191,21 @@
     def _():
         p_copy.start()
 
+    sent(p_copy, p_send)
+
     @pl.when(jnp.logical_and(tm == 0, x == 1))
     def _():
         pr[1] = psrc[...]
 
     lax.fori_loop(1, 32, send_record, 0)
+
+    def drain_record(m, carry):
+        a, b = record_copies(m)
+        a.wait_send()
+        b.wait_send()
+        return carry
+
+    drains.append(lambda: lax.fori_loop(1, 32, drain_record, 0))
 
     def gain_copy(n):
         return remote(kslab, kfull.at[pl.ds(pl.multiple_of(x * 128, 128), 128)], s_k.at[n], r_k.at[n],
@@ -155,6 +217,7 @@
 
     for n in range(1, 4):
         gain_copy(n).start()
+        sent(gain_copy(n))
     kfull[pl.ds(pl.multiple_of(x * 128, 128), 128), :] = kslab[...]
 
     acc[...] = jnp.zeros_like(acc)
@@ -201,8 +264,10 @@
     for d in range(2):
         for copy in first_copies(d):
             copy.start()
+            sent(copy)
     for copy in info_copies:
         copy.start()
+        sent(copy)
     second = [remote(hs.at[d], r2.at[d], s_2.at[d], r_2.at[d], (tm, xp)) for d in range(2)]
     third = [remote(fh.at[d], r3.at[d], s_3.at[d], r_3.at[d], (sib, x)) for d in range(2)]
     for d in range(2):
@@ -211,6 +276,7 @@
         hs[d, :, 0:512] = acc[pl.ds(d * 512 + mine, 128), :] + r1[d, :, 0:512]
         hs[d, :, 512:768] = acc[pl.ds(d * 512 + 256 + mine, 128), 256:512] + r1[d, :, 512:768]
         second[d].start()
+        sent(second[d])
     for copy in info_copies:
         copy.wait_recv()
     info = (acc[1024:1032, :] + ri[0]) + (ri[1] + ri[2])
@@ -220,7 +286,8 @@
         d_copy.wait_recv()
 
     d_rows = dl[...]
-    d_cols = d_rows.T
+    for d in range(2):
+        keep(d_tiles.at[d], to_tiles(d_rows[d:d + 1, :]))
 
     wide[0:128, :] = prop[:, pl.ds(pl.multiple_of(j * 128, 128), 128)].T * d_rows[0:1, :]
     wide[128:136, :] = jnp.zeros((8, S), F32)
@@ -228,6 +295,7 @@
         second[d].wait_recv()
         fh[d] = hs[d] + r2[d]
         third[d].start()
+        sent(third[d])
         om[d, pl.ds(mine, 128), :] = fh[d, :, 0:512]
         om[d, pl.ds(256 + mine, 128), 256:512] = fh[d, :, 512:768]
         third[d].wait_recv()
@@ -264,15 +332,21 @@
     def _():
         even_copy.start()
 
+    sent(even_copy, even_send)
+
     @pl.when(q == 1)
     def _():
         odd_copy.start()
 
+    sent(odd_copy, q == 1)
+
     brow[...] = wide[128:136, :]
 
     @pl.when(j == 0)
     def _():
         b_copy.start()
+
+    sent(b_copy, j == 0)
 
     next_g = (g + 1) % 4
     hop_copy = remote(hop_src, hop_in, s_h.at[0], r_h.at[0], (next_g * 8 + (2 * (next_g % 2)) * 2, 1))
@@ -303,6 +377,9 @@
                            (sib, x)).wait_recv()
             remote(brow, brows.at[e], s_b.at[0], r_b.at[e], (sib, x)).wait_recv()
 
+        for e in range(0, 8, 2):
+            keep(b_tiles.at[e // 2], to_tiles(brows[e, 0:1, :]))
+
         @pl.when(g > 0)
         def _():
             hop_copy.wait_recv()
@@ -310,150 +387,23 @@
         row = hop_in[0:1, :]
         for e in range(0, 8, 2):
             start_src[e] = jnp.broadcast_to(row, (8, S))
+            tiles = row_times(maps.at[e], row)
+            tiles = [tiles[k] + kept_tile(b_tiles.at[e // 2], k) for k in range(64)]
+            row = col_times(maps.at[e + 1], tiles) + brows[e + 1, 0:1, :]
+            start_src[e + 1] = jnp.broadcast_to(to_row(tiles), (8, S))
+        hop_src[...] = jnp.broadcast_to(row, (8, S))
+
+        @pl.when(g < 3)
+        def _():
+            hop_copy.start()
+
+        start_in[...] = start_src[0]
+        for e in range(7, -1, -1):
             for n in range(4):
                 if (e, n) != (0, 2):
                     start_copy(e, n).start()
-            if e == 0:
-                start_in[...] = start_src[0]
-            col = row_times(maps.at[e], row) + brows[e].T[:, 0:1]
-            row = col_times(maps.at[e + 1], col) + brows[e + 1, 0:1, :]
-            if e == 6:
-                hop_src[...] = jnp.broadcast_to(row, (8, S))
-
-                @pl.when(g < 3)
-                def _():
-                    hop_copy.start()
-            start_src[e + 1] = jnp.broadcast_to(to_row(col), (8, S))
-            for n in range(4):
-                start_copy(e + 1, n).start()
-
-    @pl.when(jnp.logical_not(is_lead))
-    def _():
-        start_copy(0, 0).wait_recv()
-
-    before = start_in[0:1, :]
-    moved = d_cols[:, 0:1] * row_times(prop, before)
-    first_col = moved - row_times(cov, col_times(om.at[0], moved) - info[0:1, :])
-    first = to_row(first_col)
-    ahead_col = row_times(prop, first)
-    moved = d_cols[:, 1:2] * ahead_col
-    second_col = moved - row_times(cov, col_times(om.at[1], moved) - info[1:2, :])
-    last = to_row(second_col)
-    msg[0:1, :] = first
-    msg[1:2, :] = last
-    msg[2:3, :] = to_row(ahead_col)
-    msg[3:4, :] = to_row(row_times(prop, last))
-    msg[4:6, :] = d_rows[0:2, :]
-    msg[6:8, :] = jnp.zeros((2, S), F32)
-
-    def mail_copy(n):
-        return remote(msg, mail.at[c_me], s_m.at[n], r_m.at[c_me], ((tm + n) % 32, j))
-
-    to_self = j == x
-
-    @pl.when(to_self)
-    def _():
-        mail[c_me] = msg[...]
-
-    @pl.when(jnp.logical_not(to_self))
-    def _():
-        mail_copy(0).start()
-
-    def post(n, carry):
-        mail_copy(n).start()
-        return carry
-
-    lax.fori_loop(1, 32, post, 0)
-
-    def wait_mail(c):
-        @pl.when(jnp.logical_not(jnp.logical_and(to_self, c == c_me)))
-        def _():
-            remote(msg, mail.at[c], s_m.at[0], r_m.at[c], (sib, x)).wait_recv()
-
-    own_cols = pl.ds(pl.multiple_of(x * 128, 128), 128)
-
-    def back(n, carry):
-        state, damp_next = carry
-        c = 31 - n
-        wait_mail(c)
-        rows = mail[c]
-        cols = rows.T
-        gap = damp_next * (state - damp_next * rows[3:4, :])
-        later = cols[:, 1:2] + row_times(kfull, gap)
-        gap_col = cols[:, 5:6] * (later - cols[:, 5:6] * cols[:, 2:3])
-        state = rows[0:1, :] + col_times(k_t, gap_col)
-
-        @pl.when(c == tm)
-        def _():
-            hs[0, 0:1, 0:512] = state
-            hs[0, 8:9, 0:512] = to_row(later)
-
-        return state, rows[4:5, :]
-
-    for d in range(2):
-        second[d].wait_send()
-    zero = jnp.zeros((1, S), F32)
-    lax.fori_loop(0, 32 - tm, back, (zero, zero))
-    smooth_out[0:1, :] = hs[0, 0:1, own_cols]
-    smooth_out[1:2, :] = hs[0, 8:9, own_cols]
-    filt_out[...] = mail[tm, 0:2, own_cols]
-
-    def drain_mail(n, carry):
-        wait_mail(n)
-        return carry
-
-    lax.fori_loop(0, tm, drain_mail, 0)
-
-    def drain_record(m, carry):
-        a, b = record_copies(m)
-        a.wait_send()
-        b.wait_send()
-        return carry
-
-    lax.fori_loop(1, 32, drain_record, 0)
-
-    def drain_post(n, carry):
-        mail_copy(n).wait_send()
-        return carry
-
-    lax.fori_loop(1, 32, drain_post, 0)
-
-    @pl.when(jnp.logical_not(to_self))
-    def _():
-        mail_copy(0).wait_send()
-
-    for n in range(1, 4):
-        gain_copy(n).wait_send()
-
-    @pl.when(jnp.logical_not(d_self))
-    def _():
-        d_copy.wait_send()
-
-    @pl.when(p_send)
-    def _():
-        p_copy.wait_send()
-
-    for d in range(2):
-        for copy in first_copies(d):
-            copy.wait_send()
-        third[d].wait_send()
-    for copy in info_copies:
-        copy.wait_send()
-
-    @pl.when(even_send)
-    def _():
-        even_copy.wait_send()
-
-    @pl.when(q == 1)
-    def _():
-        odd_copy.wait_send()
-
-    @pl.when(j == 0)
-    def _():
-        b_copy.wait_send()
-
-    @pl.when(is_lead)
-    def _():
+
+    def drain_leader():
         for e in range(8):
             for n in range(4):
                 if (e, n) != (0, 2):
@@ -462,6 +412,102 @@
         @pl.when(g < 3)
         def _():
             hop_copy.wait_send()
+
+    drains.append(lambda: pl.when(is_lead)(drain_leader))
+
+    @pl.when(jnp.logical_not(is_lead))
+    def _():
+        start_copy(0, 0).wait_recv()
+
+    before = start_in[0:1, :]
+
+    def day(d, ahead):
+        moved = [kept_tile(d_tiles.at[d], k) * ahead[k] for k in range(64)]
+        back = row_times(cov, col_times(om.at[d], moved) - info[d:d + 1, :])
+        return to_row([moved[k] - back[k] for k in range(64)])
+
+    first = day(0, row_times(prop, before))
+    ahead = row_times(prop, first)
+    last = day(1, ahead)
+    d_first, d_last = d_rows[0:1, :], d_rows[1:2, :]
+    msg[0:1, :] = first
+    msg[1:2, :] = last
+    msg[2:3, :] = d_last * (last - d_last * to_row(ahead))
+    msg[3:4, :] = to_row(row_times(prop, last))
+    msg[4:5, :] = d_first
+    msg[5:6, :] = d_last
+    msg[6:8, :] = jnp.zeros((2, S), F32)
+
+    def mail_copy(n):
+        return remote(msg, mail.at[c_me], s_m.at[n], r_m.at[c_me], (n, j))
+
+    to_self = j == x
+
+    @pl.when(to_self)
+    def _():
+        mail[c_me] = msg[...]
+
+    def to_other(n):
+        return jnp.logical_or(n != tm, jnp.logical_not(to_self))
+
+    def post(n, carry):
+        @pl.when(to_other(n))
+        def _():
+            mail_copy(n).start()
+        return carry
+
+    lax.fori_loop(0, 32, post, 0)
+
+    def drain_post(n, carry):
+        @pl.when(to_other(n))
+        def _():
+            mail_copy(n).wait_send()
+        return carry
+
+    drains.append(lambda: lax.fori_loop(0, 32, drain_post, 0))
+
+    def wait_mail(c):
+        @pl.when(jnp.logical_not(jnp.logical_and(to_self, c == c_me)))
+        def _():
+            remote(msg, mail.at[c], s_m.at[0], r_m.at[c], (sib, x)).wait_recv()
+
+    own_cols = pl.ds(pl.multiple_of(x * 128, 128), 128)
+
+    def expand(c, carry):
+        wait_mail(c)
+        keep(mail_tiles.at[c, 0], to_tiles(mail[c, 5:6, :]))
+        keep(mail_tiles.at[c, 1], to_tiles(mail[c, 2:3, :]))
+        return carry
+
+    lax.fori_loop(tm, 32, expand, 0)
+
+    def back(c, state, damp_next):
+        gap = damp_next * (state - damp_next * mail[c, 3:4, :])
+        later = row_times(kfull, gap)
+        scale, shift = mail_tiles.at[c, 0], mail_tiles.at[c, 1]
+        gaps = [kept_tile(scale, k) * later[k] + kept_tile(shift, k) for k in range(64)]
+        return mail[c, 0:1, :] + col_times(k_t, gaps), later
+
+    def back_step(n, carry):
+        state, damp_next = carry
+        c = 31 - n
+        return back(c, state, damp_next)[0], mail[c, 4:5, :]
+
+    zero = jnp.zeros((1, S), F32)
+    state, damp_next = lax.fori_loop(0, 31 - tm, back_step, (zero, zero))
+    state, later = back(tm, state, damp_next)
+    kept[0:1, :] = state
+    kept[1:2, :] = mail[tm, 1:2, :] + to_row(later)
+    smooth_out[...] = kept[0:2, own_cols]
+    filt_out[...] = mail[tm, 0:2, own_cols]
+
+    def drain_mail(n, carry):
+        wait_mail(n)
+        return carry
+
+    lax.fori_loop(0, tm, drain_mail, 0)
+    for drain in drains:
+        drain()
 
 
 def local(records, obs_values, block_day, block_count, propagator_matrix, analysis_cov, unattenuated_multiplier,
@@ -509,6 +555,10 @@
             pltpu.VMEM((8, S), F32),
             pltpu.VMEM((8, S), F32),
             pltpu.VMEM((32, 8, S), F32),
+            pltpu.VMEM((8, S), F32),
+            pltpu.VMEM((32, 2, S, 128), F32),
+            pltpu.VMEM((2, S, 128), F32),
+            pltpu.VMEM((4, S, 128), F32),
             dma((32,)), dma((32,)), dma((32,)), dma((32,)),
             dma((4,)), dma((4,)), dma((1,)), dma((1,)), dma((1,)), dma((4,)),
             dma((4,)), dma((4,)), dma((3,)), dma((3,)), dma((2,)), dma((2,)), dma((2,)), dma((2,)),

time: 184 us -> 163 us (0.89)
  Pallas kernels: 179 us -> 158 us
    pallas_call x1, Pallas kernels: 179 us -> 158 us  [local(): pl.pallas_call(kernel, out_shape=(jax.ShapeDtypeStruct((2, 128), F32), ja...]
where the time goes in v2:
time: 163 us
  Pallas kernels  158 us (97%)
  local copies, waits for them, and re-layouts  2.43 us (1%)
    pallas_call x1, Pallas kernels, local(): pl.pallas_call(kernel, out_shape=(jax.ShapeDtypeStruct((2, 128), F32), ja...  158 us

profile of v2, /device:TPU:1, one launch (start us, length us, event | category | flops | bytes accessed | tf_op | source)
XLA Modules:
  0.0 163.1 jit_solution(17831765240565610206)
XLA Ops:
  0.7 1.6 fusion.2.meta
  2.2 158.4 %shard_map.104 = (f32[2,128]{1,0:T(2,128)}, f32[2,128]{1,0:T(2,128)}) custom-call(bf16[4096,512]{1,0:T(8,128)(2,1)} %rec.1, bf16[32,16,128]{2,1,0:T(8,128)(2,1)} %fusion.2.meta, f32[512,512]{1,0:T(8,128)} %prop.1, f32[512,512]{1,0:T(8,128)} %cov.1, f32[128,512]{1,0:T(8,128)} %kslab.1, f32[2,512]{1,0:T(2,128)} %damp.1, f32[1,128]{1,0:T(1,128)} %bitcast.3), custom_call_target="tpu_custom_call" | custom-call | flops 10000000000 | bytes 100000000 | tf_op jit(solution)/shard_map/pallas_call | solution.py:523
  160.6 1.2 copy.13
  161.8 1.2 copy.14
  (3 shorter events, 0.0 us)

commit v3 on v2

--- a/solution.py
+++ b/solution.py
@@ -13,16 +13,23 @@
 
 
 def row_place(r):
-    g, i = r // 4, r % 4
+    g, i = 3 - r // 4, r % 4
     im = i % 3
-    return (2 * (g % 2) + im * (im + 1) // 2) % 4, (g + i // 3) % 4
+    return (2 * (g // 2) + im * (im + 1) // 2) % 4, g + (i // 3) * (3 - 2 * g)
 
 
 def place_row(y, z):
-    phi = (y + 2 * z) % 4
-    i = phi + (phi // 2) * (5 - 2 * phi)
-    g = (z - i // 3 + 4) % 4
-    return g, i
+    odd = y % 2
+    extra = (1 - odd) * ((y // 2 + z // 2) % 2)
+    g = z + extra * (3 - 2 * z)
+    return 3 - g, odd * (1 + ((y - 2 * (z // 2) + 4) % 4) // 2) + 3 * extra
+
+
+def lead_of(g):
+    return (3 - g) * 8 + (3 - g) // 2 * 4
+
+
+PARTS = (((0, 0, 512, 0), (3, 384, 128, 512)), ((1, 128, 384, 0), (2, 256, 256, 384)))
 
 
 def row_times(ref, row):
@@ -89,11 +96,11 @@
     return lax.dot_general(a, b, (((1,), (1,)), ((), ())), precision=HIGH, preferred_element_type=F32)
 
 
-def kernel(rec, meta, prop, cov, kslab, damp, prior, filt_out, smooth_out,
+def kernel(rec, meta, prop_in, cov_in, kslab_in, damp, prior, filt_out, smooth_out,
            land, mland, lhs, acc, r1, hs, r2, fh, r3, ri, om, wide, slab, slab_t, brow, maps, brows, kfull, k_t,
            dsrc, dl, psrc, pr, hop_src, hop_in, start_src, start_in, msg, mail, kept, mail_tiles, d_tiles, b_tiles,
            s_rec, r_rec, s_meta, r_meta, s_k, r_k, s_d, r_d, s_p, r_p, s_1, r_1, s_i, r_i, s_2, r_2, s_3, r_3,
-           s_a, r_a, s_b, r_b, s_h, r_h, s_s, r_s, s_m, r_m, l_rec, l_meta):
+           s_a, r_a, s_b, r_b, s_h, r_h, s_s, r_s, s_m, r_m, l_rec, l_meta, prop, cov, kslab, l_in):
     tm, x = lax.axis_index("tm"), lax.axis_index("obs")
     z, y, core = tm // 8, (tm // 2) % 4, tm % 2
     q, xi = x // 2, x % 2
@@ -101,7 +108,7 @@
     e_me = 2 * i_row + q
     c_me = 8 * g + e_me
     j = 2 * xi + core
-    lead_tm = g * 8 + (2 * (g % 2)) * 2
+    lead_tm = lead_of(g)
     is_lead = jnp.logical_and(tm == lead_tm, x == 1)
     sib = tm + 1 - 2 * core
     xp = x + 1 - 2 * xi
@@ -136,10 +143,15 @@
         greet(owner_of(o)[1])
         return carry
 
+    loads = [pltpu.make_async_copy(a, b, l_in.at[n])
+             for n, (a, b) in enumerate(((prop_in, prop), (cov_in, cov), (kslab_in, kslab)))]
     lax.fori_loop(1, 32, greet_source, 0)
     for dev in ((tm, (x + 1) % 4), (tm, (x + 2) % 4), (tm, (x + 3) % 4), (sib, x), (sib, xp),
                 (c_me, 2 * xi + core)):
         greet(dev)
+    for load in loads:
+        load.start()
+    acc[...] = jnp.zeros_like(acc)
     pl.semaphore_wait(barrier, 37)
 
     def offset(m):
@@ -183,20 +195,6 @@
 
     sent(d_copy, jnp.logical_not(d_self))
 
-    psrc[...] = jnp.broadcast_to(prior[...], (8, 128))
-    p_copy = remote(psrc, pr.at[x], s_p.at[0], r_p.at[x], (0, 1))
-    p_send = jnp.logical_and(tm == 0, x != 1)
-
-    @pl.when(p_send)
-    def _():
-        p_copy.start()
-
-    sent(p_copy, p_send)
-
-    @pl.when(jnp.logical_and(tm == 0, x == 1))
-    def _():
-        pr[1] = psrc[...]
-
     lax.fori_loop(1, 32, send_record, 0)
 
     def drain_record(m, carry):
@@ -207,20 +205,8 @@
 
     drains.append(lambda: lax.fori_loop(1, 32, drain_record, 0))
 
-    def gain_copy(n):
-        return remote(kslab, kfull.at[pl.ds(pl.multiple_of(x * 128, 128), 128)], s_k.at[n], r_k.at[n],
-                      (tm, (x + n) % 4))
-
-    def gain_in(n):
-        ox = (x - n + 4) % 4
-        return remote(kslab, kfull.at[pl.ds(pl.multiple_of(ox * 128, 128), 128)], s_k.at[n], r_k.at[n], (tm, xp))
-
-    for n in range(1, 4):
-        gain_copy(n).start()
-        sent(gain_copy(n))
-    kfull[pl.ds(pl.multiple_of(x * 128, 128), 128), :] = kslab[...]
-
-    acc[...] = jnp.zeros_like(acc)
+    for load in loads:
+        load.wait()
     own_rec.wait()
     own_meta.wait()
 
@@ -245,36 +231,43 @@
 
     lax.fori_loop(0, 16, gram, 0)
 
-    for n in range(1, 4):
-        gain_in(n).wait_recv()
-    k_t[...] = kfull[...].T
-
-    mine, theirs = pl.multiple_of(128 * core, 128), pl.multiple_of(128 * (1 - core), 128)
-
-    def first_copies(d):
-        return (
-            remote(acc.at[pl.ds(d * 512 + theirs, 128), :], r1.at[d, :, pl.ds(0, 512)], s_1.at[2 * d], r_1.at[2 * d],
-                   (sib, x)),
-            remote(acc.at[pl.ds(d * 512 + 256 + theirs, 128), pl.ds(256, 256)], r1.at[d, :, pl.ds(512, 256)],
-                   s_1.at[2 * d + 1], r_1.at[2 * d + 1], (sib, x)),
-        )
+    def first_copies(d, owner):
+        return [remote(acc.at[pl.ds(d * 512 + 128 * r, 128), pl.ds(c0, w)], r1.at[d, :, pl.ds(at, w)],
+                       s_1.at[2 * d + n], r_1.at[2 * d + n], (sib, x))
+                for n, (r, c0, w, at) in enumerate(PARTS[owner])]
+
+    def by_core(step):
+        for own in range(2):
+            pl.when(core == own)(lambda own=own: step(own))
 
     peers = ((sib, x), (tm, xp), (sib, xp))
     info_copies = [remote(acc.at[pl.ds(1024, 8), :], ri.at[n], s_i.at[n], r_i.at[n], peers[n]) for n in range(3)]
-    for d in range(2):
-        for copy in first_copies(d):
-            copy.start()
-            sent(copy)
+    def give(own):
+        for d in range(2):
+            for copy in first_copies(d, 1 - own):
+                copy.start()
+
+    def given(own):
+        for d in range(2):
+            for copy in first_copies(d, 1 - own):
+                copy.wait_send()
+
+    by_core(give)
+    drains.append(lambda: by_core(given))
     for copy in info_copies:
         copy.start()
         sent(copy)
     second = [remote(hs.at[d], r2.at[d], s_2.at[d], r_2.at[d], (tm, xp)) for d in range(2)]
     third = [remote(fh.at[d], r3.at[d], s_3.at[d], r_3.at[d], (sib, x)) for d in range(2)]
     for d in range(2):
-        for copy in first_copies(d):
-            copy.wait_recv()
-        hs[d, :, 0:512] = acc[pl.ds(d * 512 + mine, 128), :] + r1[d, :, 0:512]
-        hs[d, :, 512:768] = acc[pl.ds(d * 512 + 256 + mine, 128), 256:512] + r1[d, :, 512:768]
+        def add(own, d=d):
+            for copy in first_copies(d, own):
+                copy.wait_recv()
+            for r, c0, w, at in PARTS[own]:
+                hs[d, :, at:at + w] = (acc[d * 512 + 128 * r:d * 512 + 128 * r + 128, c0:c0 + w]
+                                       + r1[d, :, at:at + w])
+
+        by_core(add)
         second[d].start()
         sent(second[d])
     for copy in info_copies:
@@ -296,12 +289,17 @@
         fh[d] = hs[d] + r2[d]
         third[d].start()
         sent(third[d])
-        om[d, pl.ds(mine, 128), :] = fh[d, :, 0:512]
-        om[d, pl.ds(256 + mine, 128), 256:512] = fh[d, :, 512:768]
+        def put(own, src, d=d):
+            for r, c0, w, at in PARTS[own]:
+                om[d, 128 * r:128 * r + 128, c0:c0 + w] = src[d, :, at:at + w]
+
+        by_core(lambda own: put(own, fh))
         third[d].wait_recv()
-        om[d, pl.ds(theirs, 128), :] = r3[d, :, 0:512]
-        om[d, pl.ds(256 + theirs, 128), 256:512] = r3[d, :, 512:768]
-        om[d, 256:512, 0:256] = om[d, 0:256, 256:512].T
+        by_core(lambda own: put(1 - own, r3))
+        for r in range(1, 4):
+            for c in range(r):
+                om[d, 128 * r:128 * r + 128, 128 * c:128 * c + 128] = (
+                    om[d, 128 * c:128 * c + 128, 128 * r:128 * r + 128].T)
         if d == 1:
             wide[...] = dot_nt(wide[...], prop[...]) * d_rows[1:2, :]
         w = wide[...]
@@ -348,8 +346,39 @@
 
     sent(b_copy, j == 0)
 
+    psrc[...] = jnp.broadcast_to(prior[...], (8, 128))
+    p_copy = remote(psrc, pr.at[x], s_p.at[0], r_p.at[x], (lead_of(0), 1))
+    p_send = jnp.logical_and(tm == lead_of(0), x != 1)
+
+    @pl.when(p_send)
+    def _():
+        p_copy.start()
+
+    sent(p_copy, p_send)
+
+    @pl.when(jnp.logical_and(tm == lead_of(0), x == 1))
+    def _():
+        pr[1] = psrc[...]
+
+    def gain_copy(n):
+        return remote(kslab, kfull.at[pl.ds(pl.multiple_of(x * 128, 128), 128)], s_k.at[n], r_k.at[n],
+                      (tm, (x + n) % 4))
+
+    def gain_in(n):
+        ox = (x - n + 4) % 4
+        return remote(kslab, kfull.at[pl.ds(pl.multiple_of(ox * 128, 128), 128)], s_k.at[n], r_k.at[n], (tm, xp))
+
+    for n in range(1, 4):
+        gain_copy(n).start()
+        sent(gain_copy(n))
+    kfull[pl.ds(pl.multiple_of(x * 128, 128), 128), :] = kslab[...]
+
+    for n in range(1, 4):
+        gain_in(n).wait_recv()
+    k_t[...] = kfull[...].T
+
     next_g = (g + 1) % 4
-    hop_copy = remote(hop_src, hop_in, s_h.at[0], r_h.at[0], (next_g * 8 + (2 * (next_g % 2)) * 2, 1))
+    hop_copy = remote(hop_src, hop_in, s_h.at[0], r_h.at[0], (lead_of(next_g), 1))
 
     def start_copy(e, n):
         sy, sz = row_place(4 * g + e // 2)
@@ -361,7 +390,7 @@
         @pl.when(g == 0)
         def _():
             for ox in (0, 2, 3):
-                remote(psrc, pr.at[ox], s_p.at[0], r_p.at[ox], (0, 0)).wait_recv()
+                remote(psrc, pr.at[ox], s_p.at[0], r_p.at[ox], (sib, x)).wait_recv()
             for ox in range(4):
                 hop_in[:, 128 * ox:128 * ox + 128] = pr[ox]
 
@@ -510,6 +539,11 @@
         drain()
 
 
+def hand_out(filt, smooth, filt_out, smooth_out):
+    filt_out[...] = filt[...]
+    smooth_out[...] = smooth[...]
+
+
 def local(records, obs_values, block_day, block_count, propagator_matrix, analysis_cov, unattenuated_multiplier,
           damping, prior_mean):
     slot = lax.broadcasted_iota(jnp.int32, (32, 16, 128), 2)
@@ -519,22 +553,23 @@
     values = jnp.where(part < 2, obs_values.reshape(32, 1, 128), jnp.ones((), BF16))
     meta = jnp.where(held, values, jnp.zeros((), BF16))
     vmem = pl.BlockSpec(memory_space=pltpu.VMEM)
+    hbm = pl.BlockSpec(memory_space=pl.ANY)
     dma = pltpu.SemaphoreType.DMA
-    return pl.pallas_call(
+    results = pl.pallas_call(
         kernel,
         out_shape=(jax.ShapeDtypeStruct((2, 128), F32), jax.ShapeDtypeStruct((2, 128), F32)),
-        in_specs=[pl.BlockSpec(memory_space=pl.ANY)] + [vmem] * 6,
+        in_specs=[hbm] * 5 + [vmem] * 2,
         out_specs=(vmem, vmem),
         scratch_shapes=[
             pltpu.VMEM((16, 256, S), BF16),
             pltpu.VMEM((32, 16, 128), BF16),
             pltpu.VMEM((1040, 256), BF16),
             pltpu.VMEM((1040, S), F32),
-            pltpu.VMEM((2, 128, 768), F32),
-            pltpu.VMEM((2, 128, 768), F32),
-            pltpu.VMEM((2, 128, 768), F32),
-            pltpu.VMEM((2, 128, 768), F32),
-            pltpu.VMEM((2, 128, 768), F32),
+            pltpu.VMEM((2, 128, 640), F32),
+            pltpu.VMEM((2, 128, 640), F32),
+            pltpu.VMEM((2, 128, 640), F32),
+            pltpu.VMEM((2, 128, 640), F32),
+            pltpu.VMEM((2, 128, 640), F32),
             pltpu.VMEM((3, 8, S), F32),
             pltpu.VMEM((2, S, S), F32),
             pltpu.VMEM((136, S), F32),
@@ -564,10 +599,17 @@
             dma((4,)), dma((4,)), dma((3,)), dma((3,)), dma((2,)), dma((2,)), dma((2,)), dma((2,)),
             dma((1,)), dma((32,)), dma((1,)), dma((8,)), dma((1,)), dma((1,)),
             dma((32,)), dma((1,)), dma((32,)), dma((32,)), dma, dma,
+            pltpu.VMEM((S, S), F32), pltpu.VMEM((S, S), F32), pltpu.VMEM((128, S), F32), dma((3,)),
         ],
         compiler_params=pltpu.CompilerParams(collective_id=0, has_side_effects=True, vmem_limit_bytes=56 << 20),
         cost_estimate=pl.CostEstimate(flops=10**10, bytes_accessed=10**8, transcendentals=0),
     )(records, meta, propagator_matrix, analysis_cov, unattenuated_multiplier, damping, prior_mean.reshape(1, 128))
+    return pl.pallas_call(
+        hand_out,
+        out_shape=(jax.ShapeDtypeStruct((2, 128), F32), jax.ShapeDtypeStruct((2, 128), F32)),
+        in_specs=[vmem, vmem],
+        out_specs=(vmem, vmem),
+    )(*results)
 
 
 def solution(mesh):

time: 163 us -> 151 us (0.926)
  Pallas kernels: 158 us -> 148 us
  local copies, waits for them, and re-layouts: 2.43 us -> 0 us
    pallas_call x1, Pallas kernels: 158 us -> 147 us  [local(): pl.pallas_call(kernel, out_shape=(jax.ShapeDtypeStruct((2, 128), F32), ja...]
    unnamed x2 -> x0, local copies, waits for them, and re-layouts: 2.43 us -> none
where the time goes in v3:
time: 151 us
  Pallas kernels  148 us (98%)
  other arithmetic  1.58 us (1%)
    pallas_call x1, Pallas kernels, local(): pl.pallas_call(kernel, out_shape=(jax.ShapeDtypeStruct((2, 128), F32), ja...  147 us

profile of v3, /device:TPU:1, one launch (start us, length us, event | category | flops | bytes accessed | tf_op | source)
XLA Modules:
  0.0 150.5 jit_solution(14452698347932488328)
XLA Ops:
  0.7 1.6 %fusion.2.meta = bf16[32,16,128]{2,1,0:T(8,128)(2,1)} fusion(s32[16]{0:T(128)S(1)} %get-tuple-element.8, s32[16]{0:T(128)S(1)} %get-tuple-element.9, s32[32]{0:T(128)} %param.11, s32[32]{0:T(128)} %param.12, pred[16]{0:T(512)(128)(4,1)S(1)} %get-tuple-element.7, pred[16]{0:T(512)(128)(4,1)S(1)} %iota_compare_fusion.2, pred[16]{0:T(512)(128)(4,1)S(1)} %get-tuple-element.6, ...), kind=kLoop, calls=%fused_computation.4 | loop fusion | flops 458752 | bytes 139696 | tf_op jit(solution)/shard_map/jit(_where)/select_n | solution.py:554
  2.2 147.1 %shard_map.104 = (f32[2,128]{1,0:T(2,128)}, f32[2,128]{1,0:T(2,128)}) custom-call(bf16[4096,512]{1,0:T(8,128)(2,1)} %rec.1, bf16[32,16,128]{2,1,0:T(8,128)(2,1)} %fusion.2.meta, f32[512,512]{1,0:T(8,128)} %prop_in.1, f32[512,512]{1,0:T(8,128)} %cov_in.1, f32[128,512]{1,0:T(8,128)} %kslab_in.1, f32[2,512]{1,0:T(2,128)} %damp.1, f32[1,128]{1,0:T(1,128)} %bitcast.3), custom_call_target="tpu_custom_call" | custom-call | flops 10000000000 | bytes 100000000 | tf_op jit(solution)/shard_map/pallas_call | solution.py:558
  149.3 1.2 shard_map.105
  (3 shorter events, 0.0 us)

commit v4 on v3

--- a/solution.py
+++ b/solution.py
@@ -8,12 +8,11 @@
 MESH = pl.DeviceIdType.MESH
 F32 = jnp.float32
 BF16 = jnp.bfloat16
-HIGH = lax.Precision.HIGHEST
 S = 512
 
 
 def row_place(r):
-    g, i = 3 - r // 4, r % 4
+    g, i = r // 4, r % 4
     im = i % 3
     return (2 * (g // 2) + im * (im + 1) // 2) % 4, g + (i // 3) * (3 - 2 * g)
 
@@ -22,11 +21,11 @@
     odd = y % 2
     extra = (1 - odd) * ((y // 2 + z // 2) % 2)
     g = z + extra * (3 - 2 * z)
-    return 3 - g, odd * (1 + ((y - 2 * (z // 2) + 4) % 4) // 2) + 3 * extra
+    return g, odd * (1 + ((y - 2 * (z // 2) + 4) % 4) // 2) + 3 * extra
 
 
 def lead_of(g):
-    return (3 - g) * 8 + (3 - g) // 2 * 4
+    return g * 8 + g // 2 * 4
 
 
 PARTS = (((0, 0, 512, 0), (3, 384, 128, 512)), ((1, 128, 384, 0), (2, 256, 256, 384)))
@@ -88,19 +87,26 @@
     return ref[8 * k:8 * k + 8, :]
 
 
-def dot(a, b):
-    return jnp.dot(a, b, precision=HIGH, preferred_element_type=F32)
-
-
-def dot_nt(a, b):
-    return lax.dot_general(a, b, (((1,), (1,)), ((), ())), precision=HIGH, preferred_element_type=F32)
-
-
-def kernel(rec, meta, prop_in, cov_in, kslab_in, damp, prior, filt_out, smooth_out,
+def parts_of(a):
+    high = a.astype(BF16)
+    return high, (a - high.astype(F32)).astype(BF16)
+
+
+def dot(a, parts):
+    high, low = parts_of(a)
+    b_high, b_low = parts
+
+    def product(u, v):
+        return jnp.dot(u, v, preferred_element_type=F32)
+
+    return product(high, b_high) + (product(high, b_low) + product(low, b_high))
+
+
+def kernel(rec, values, days, counts, prop_in, cov_in, kslab_in, damp, prior, filt_out, smooth_out,
            land, mland, lhs, acc, r1, hs, r2, fh, r3, ri, om, wide, slab, slab_t, brow, maps, brows, kfull, k_t,
            dsrc, dl, psrc, pr, hop_src, hop_in, start_src, start_in, msg, mail, kept, mail_tiles, d_tiles, b_tiles,
            s_rec, r_rec, s_meta, r_meta, s_k, r_k, s_d, r_d, s_p, r_p, s_1, r_1, s_i, r_i, s_2, r_2, s_3, r_3,
-           s_a, r_a, s_b, r_b, s_h, r_h, s_s, r_s, s_m, r_m, l_rec, l_meta, prop, cov, kslab, l_in):
+           s_a, r_a, s_b, r_b, s_h, r_h, s_s, r_s, s_m, r_m, l_rec, prop, cov, kslab, l_in, meta, plain, s_w, r_w, s_r, pt_parts, c_parts):
     tm, x = lax.axis_index("tm"), lax.axis_index("obs")
     z, y, core = tm // 8, (tm // 2) % 4, tm % 2
     q, xi = x // 2, x % 2
@@ -151,6 +157,16 @@
         greet(dev)
     for load in loads:
         load.start()
+    slot = lax.broadcasted_iota(jnp.int32, (16, 128), 1)
+    part = lax.broadcasted_iota(jnp.int32, (16, 128), 0)
+    plain[...] = values[...].astype(F32)
+
+    def mark(c):
+        held = jnp.logical_and(jnp.logical_and(slot < counts[c], part % 2 == days[c]), part < 4)
+        filled = jnp.where(part < 2, jnp.broadcast_to(plain[pl.ds(c, 1), :], (16, 128)), 1.0)
+        return jnp.where(held, filled, 0.0).astype(BF16)
+
+    mland[0] = mark(c_me)
     acc[...] = jnp.zeros_like(acc)
     pl.semaphore_wait(barrier, 37)
 
@@ -163,7 +179,7 @@
         tg, ti = place_row(ty, tz)
         c = 8 * tg + 2 * ti + tq
         dev = (tz * 8 + ty * 2 + core, tx)
-        return (
+        return c, (
             remote(rec.at[pl.ds(pl.multiple_of(c * 128, 128), 128)],
                    land.at[m // 2, pl.ds(pl.multiple_of((m % 2) * 128, 128), 128)], s_rec.at[m], r_rec.at[m], dev),
             remote(meta.at[c], mland.at[m], s_meta.at[m], r_meta.at[m], dev),
@@ -172,13 +188,11 @@
     own_rec = pltpu.make_async_copy(rec.at[pl.ds(pl.multiple_of(c_me * 128, 128), 128)],
                                     land.at[0, pl.ds(0, 128)], l_rec)
     own_rec.start()
-    own_meta = pltpu.make_async_copy(meta.at[c_me], mland.at[0], l_meta)
-    own_meta.start()
-
     def send_record(m, carry):
-        a, b = record_copies(m)
+        c, (a, b) = record_copies(m)
+        a.start()
+        meta[c] = mark(c)
         b.start()
-        a.start()
         return carry
 
     dsrc[...] = jnp.zeros_like(dsrc)
@@ -196,22 +210,40 @@
     sent(d_copy, jnp.logical_not(d_self))
 
     lax.fori_loop(1, 32, send_record, 0)
+    loads[2].wait()
+    def gain_rows(ox, half):
+        return pl.ds(pl.multiple_of(ox * 128 + half * 64, 64), 64)
+
+    half_slab = kslab.at[pl.ds(pl.multiple_of(core * 64, 64), 64)]
+
+    def gain_copy(n, ox):
+        return remote(half_slab, kfull.at[gain_rows(ox, core)], s_k.at[n], r_k.at[n], (tm, (x + n) % 4))
+
+    def gain_swap(n, half):
+        rows = gain_rows((x - n + 4) % 4, half)
+        return remote(kfull.at[rows], kfull.at[rows], s_w.at[n], r_w.at[n], (sib, x))
+
+    for n in range(1, 4):
+        gain_copy(n, x).start()
+        sent(gain_copy(n, x))
+    kfull[pl.ds(pl.multiple_of(x * 128, 128), 128), :] = kslab[...]
 
     def drain_record(m, carry):
-        a, b = record_copies(m)
+        a, b = record_copies(m)[1]
         a.wait_send()
         b.wait_send()
         return carry
 
     drains.append(lambda: lax.fori_loop(1, 32, drain_record, 0))
 
-    for load in loads:
+    for load in loads[:2]:
         load.wait()
+    pt_parts[0], pt_parts[1] = parts_of(prop[...].T)
+    c_parts[0], c_parts[1] = parts_of(cov[...])
     own_rec.wait()
-    own_meta.wait()
 
     def wait_record(m):
-        a, b = record_copies(m)
+        a, b = record_copies(m)[1]
         b.wait_recv()
         a.wait_recv()
 
@@ -301,15 +333,17 @@
                 om[d, 128 * r:128 * r + 128, 128 * c:128 * c + 128] = (
                     om[d, 128 * c:128 * c + 128, 128 * r:128 * r + 128].T)
         if d == 1:
-            wide[...] = dot_nt(wide[...], prop[...]) * d_rows[1:2, :]
+            wide[...] = dot(wide[...], (pt_parts[0], pt_parts[1])) * d_rows[1:2, :]
         w = wide[...]
         seen = jnp.concatenate([jnp.zeros((128, S), F32), jnp.broadcast_to(info[d:d + 1, :], (8, S))], axis=0)
-        wide[...] = w - dot(dot(w, om[d]) - seen, cov[...])
+        wide[...] = w - dot(dot(w, parts_of(om[d])) - seen, (c_parts[0], c_parts[1]))
 
     lead = (lead_tm, 1)
+    by_row = jnp.logical_and(xi == 0, (1 - q) * (i_row + 1) // 2 % 2 + q * i_row // 3 == 1)
+    to_lead = (lead_tm + jnp.where(by_row, core, 0), jnp.where(by_row, x, 1))
     slab_cols = pl.multiple_of(j * 128, 128)
-    even_copy = remote(slab_t, maps.at[e_me, :, pl.ds(slab_cols, 128)], s_a.at[0], r_a.at[e_me * 4 + j], lead)
-    odd_copy = remote(slab, maps.at[e_me, pl.ds(slab_cols, 128), :], s_a.at[0], r_a.at[e_me * 4 + j], lead)
+    even_copy = remote(slab_t, maps.at[e_me, :, pl.ds(slab_cols, 128)], s_a.at[0], r_a.at[e_me * 4 + j], to_lead)
+    odd_copy = remote(slab, maps.at[e_me, pl.ds(slab_cols, 128), :], s_a.at[0], r_a.at[e_me * 4 + j], to_lead)
     b_copy = remote(brow, brows.at[e_me], s_b.at[0], r_b.at[e_me], lead)
 
     @pl.when(q == 0)
@@ -360,22 +394,49 @@
     def _():
         pr[1] = psrc[...]
 
-    def gain_copy(n):
-        return remote(kslab, kfull.at[pl.ds(pl.multiple_of(x * 128, 128), 128)], s_k.at[n], r_k.at[n],
-                      (tm, (x + n) % 4))
-
-    def gain_in(n):
-        ox = (x - n + 4) % 4
-        return remote(kslab, kfull.at[pl.ds(pl.multiple_of(ox * 128, 128), 128)], s_k.at[n], r_k.at[n], (tm, xp))
+    def pass_on(e):
+        if e % 2 == 0:
+            place = maps.at[e, :, pl.ds(slab_cols, 128)]
+        else:
+            place = maps.at[e, pl.ds(slab_cols, 128), :]
+        return remote(place, place, s_r.at[e], r_a.at[e * 4 + j], lead)
+
+    in_middle = jnp.logical_and(i_row == 0, xi == 0)
+    for at_q, passed in ((0, (2, 4)), (1, (7,))):
+        relays = jnp.logical_and(in_middle, q == at_q)
+
+        @pl.when(relays)
+        def _(passed=passed):
+            for e in passed:
+                pass_on(e).wait_recv()
+                pass_on(e).start()
+
+        for e in passed:
+            sent(pass_on(e), relays)
 
     for n in range(1, 4):
-        gain_copy(n).start()
-        sent(gain_copy(n))
-    kfull[pl.ds(pl.multiple_of(x * 128, 128), 128), :] = kslab[...]
-
+        gain_copy(n, (x - n + 4) % 4).wait_recv()
+        gain_swap(n, core).start()
+        sent(gain_swap(n, core))
     for n in range(1, 4):
-        gain_in(n).wait_recv()
+        gain_swap(n, 1 - core).wait_recv()
     k_t[...] = kfull[...].T
+
+    to_self = j == x
+
+    def wait_mail(c):
+        @pl.when(jnp.logical_not(jnp.logical_and(to_self, c == c_me)))
+        def _():
+            remote(msg, mail.at[c], s_m.at[0], r_m.at[c], (sib, x)).wait_recv()
+
+    def expand(c, carry):
+        wait_mail(c)
+        keep(mail_tiles.at[c, 0], to_tiles(mail[c, 5:6, :]))
+        keep(mail_tiles.at[c, 1], to_tiles(mail[c, 2:3, :]))
+        return carry
+
+    early_end = jnp.maximum(tm, 8 * (g - 1))
+    early_lead = jnp.maximum(tm, 8 * (g - 2))
 
     next_g = (g + 1) % 4
     hop_copy = remote(hop_src, hop_in, s_h.at[0], r_h.at[0], (lead_of(next_g), 1))
@@ -409,6 +470,8 @@
         for e in range(0, 8, 2):
             keep(b_tiles.at[e // 2], to_tiles(brows[e, 0:1, :]))
 
+        lax.fori_loop(tm, early_lead, expand, 0)
+
         @pl.when(g > 0)
         def _():
             hop_copy.wait_recv()
@@ -443,6 +506,8 @@
             hop_copy.wait_send()
 
     drains.append(lambda: pl.when(is_lead)(drain_leader))
+
+    lax.fori_loop(jnp.where(is_lead, early_lead, tm), early_end, expand, 0)
 
     @pl.when(jnp.logical_not(is_lead))
     def _():
@@ -470,8 +535,6 @@
     def mail_copy(n):
         return remote(msg, mail.at[c_me], s_m.at[n], r_m.at[c_me], (n, j))
 
-    to_self = j == x
-
     @pl.when(to_self)
     def _():
         mail[c_me] = msg[...]
@@ -495,20 +558,9 @@
 
     drains.append(lambda: lax.fori_loop(0, 32, drain_post, 0))
 
-    def wait_mail(c):
-        @pl.when(jnp.logical_not(jnp.logical_and(to_self, c == c_me)))
-        def _():
-            remote(msg, mail.at[c], s_m.at[0], r_m.at[c], (sib, x)).wait_recv()
-
     own_cols = pl.ds(pl.multiple_of(x * 128, 128), 128)
 
-    def expand(c, carry):
-        wait_mail(c)
-        keep(mail_tiles.at[c, 0], to_tiles(mail[c, 5:6, :]))
-        keep(mail_tiles.at[c, 1], to_tiles(mail[c, 2:3, :]))
-        return carry
-
-    lax.fori_loop(tm, 32, expand, 0)
+    lax.fori_loop(early_end, 32, expand, 0)
 
     def back(c, state, damp_next):
         gap = damp_next * (state - damp_next * mail[c, 3:4, :])
@@ -546,19 +598,14 @@
 
 def local(records, obs_values, block_day, block_count, propagator_matrix, analysis_cov, unattenuated_multiplier,
           damping, prior_mean):
-    slot = lax.broadcasted_iota(jnp.int32, (32, 16, 128), 2)
-    part = lax.broadcasted_iota(jnp.int32, (32, 16, 128), 1)
-    held = jnp.logical_and(slot < block_count[:, None, None], block_day[:, None, None] == part % 2)
-    held = jnp.logical_and(held, part < 4)
-    values = jnp.where(part < 2, obs_values.reshape(32, 1, 128), jnp.ones((), BF16))
-    meta = jnp.where(held, values, jnp.zeros((), BF16))
     vmem = pl.BlockSpec(memory_space=pltpu.VMEM)
     hbm = pl.BlockSpec(memory_space=pl.ANY)
+    smem = pl.BlockSpec(memory_space=pltpu.SMEM)
     dma = pltpu.SemaphoreType.DMA
     results = pl.pallas_call(
         kernel,
         out_shape=(jax.ShapeDtypeStruct((2, 128), F32), jax.ShapeDtypeStruct((2, 128), F32)),
-        in_specs=[hbm] * 5 + [vmem] * 2,
+        in_specs=[hbm, vmem, smem, smem] + [hbm] * 3 + [vmem] * 2,
         out_specs=(vmem, vmem),
         scratch_shapes=[
             pltpu.VMEM((16, 256, S), BF16),
@@ -598,12 +645,16 @@
             dma((4,)), dma((4,)), dma((1,)), dma((1,)), dma((1,)), dma((4,)),
             dma((4,)), dma((4,)), dma((3,)), dma((3,)), dma((2,)), dma((2,)), dma((2,)), dma((2,)),
             dma((1,)), dma((32,)), dma((1,)), dma((8,)), dma((1,)), dma((1,)),
-            dma((32,)), dma((1,)), dma((32,)), dma((32,)), dma, dma,
+            dma((32,)), dma((1,)), dma((32,)), dma((32,)), dma,
             pltpu.VMEM((S, S), F32), pltpu.VMEM((S, S), F32), pltpu.VMEM((128, S), F32), dma((3,)),
+            pltpu.VMEM((32, 16, 128), BF16),
+            pltpu.VMEM((32, 128), F32),
+            dma((4,)), dma((4,)), dma((8,)),
+            pltpu.VMEM((2, S, S), BF16), pltpu.VMEM((2, S, S), BF16),
         ],
         compiler_params=pltpu.CompilerParams(collective_id=0, has_side_effects=True, vmem_limit_bytes=56 << 20),
         cost_estimate=pl.CostEstimate(flops=10**10, bytes_accessed=10**8, transcendentals=0),
-    )(records, meta, propagator_matrix, analysis_cov, unattenuated_multiplier, damping, prior_mean.reshape(1, 128))
+    )(records, obs_values.reshape(32, 128), block_day, block_count, propagator_matrix, analysis_cov, unattenuated_multiplier, damping, prior_mean.reshape(1, 128))
     return pl.pallas_call(
         hand_out,
         out_shape=(jax.ShapeDtypeStruct((2, 128), F32), jax.ShapeDtypeStruct((2, 128), F32)),

time: 151 us -> 145 us (0.960)
  Pallas kernels: 148 us -> 144 us
  other arithmetic: 1.58 us -> 0 us
    pallas_call x1, Pallas kernels: 147 us -> 143 us  [local(): pl.pallas_call(kernel, out_shape=(jax.ShapeDtypeStruct((2, 128), F32), ja...]
    select_n x1 -> x0, other arithmetic: 1.56 us -> none  [local(): meta = jnp.where(held, values, jnp.zeros((), BF16))]
where the time goes in v4:
time: 145 us; the launch traced here: 144 us
  Pallas kernels  144 us (99%)
    pallas_call x1, Pallas kernels, local(): pl.pallas_call(kernel, out_shape=(jax.ShapeDtypeStruct((2, 128), F32), ja...  143 us

profile of v4, /device:TPU:1, one launch (start us, length us, event | category | flops | bytes accessed | tf_op | source)
XLA Modules:
  0.0 144.5 jit_solution(12567307841385915598)
XLA Ops:
  0.6 142.6 %shard_map.104 = (f32[2,128]{1,0:T(2,128)}, f32[2,128]{1,0:T(2,128)}) custom-call(bf16[4096,512]{1,0:T(8,128)(2,1)} %rec.1, bf16[32,128]{1,0:T(8,128)(2,1)} %bitcast.2, s32[32]{0:T(128)} %days.1, s32[32]{0:T(128)} %counts.1, f32[512,512]{1,0:T(8,128)} %prop_in.1, f32[512,512]{1,0:T(8,128)} %cov_in.1, f32[128,512]{1,0:T(8,128)} %kslab_in.1, f32[2,512]{1,0:T(2,128)} %damp.1, ...), custom_call_target="tpu_custom_call" | custom-call | flops 10000000000 | bytes 100000000 | tf_op jit(solution)/shard_map/pallas_call | solution.py:605
  143.2 1.2 shard_map.105

commit v5 on v4

--- a/solution.py
+++ b/solution.py
@@ -481,14 +481,17 @@
             start_src[e] = jnp.broadcast_to(row, (8, S))
             tiles = row_times(maps.at[e], row)
             tiles = [tiles[k] + kept_tile(b_tiles.at[e // 2], k) for k in range(64)]
+            keep(b_tiles.at[e // 2], tiles)
             row = col_times(maps.at[e + 1], tiles) + brows[e + 1, 0:1, :]
-            start_src[e + 1] = jnp.broadcast_to(to_row(tiles), (8, S))
         hop_src[...] = jnp.broadcast_to(row, (8, S))
 
         @pl.when(g < 3)
         def _():
             hop_copy.start()
 
+        for e in range(7, 0, -2):
+            start_src[e] = jnp.broadcast_to(
+                to_row([kept_tile(b_tiles.at[e // 2], k) for k in range(64)]), (8, S))
         start_in[...] = start_src[0]
         for e in range(7, -1, -1):
             for n in range(4):

time: 145 us -> 144 us (level)
  no operation moved by 1% of the time
where the time goes in v5:
time: 144 us
  Pallas kernels  144 us (100%)
    pallas_call x1, Pallas kernels, local(): pl.pallas_call(kernel, out_shape=(jax.ShapeDtypeStruct((2, 128), F32), ja...  142 us

profile of v5, /device:TPU:1, one launch (start us, length us, event | category | flops | bytes accessed | tf_op | source)
XLA Modules:
  0.0 144.3 jit_solution(10905392818525154381)
XLA Ops:
  0.6 142.4 %shard_map.104 = (f32[2,128]{1,0:T(2,128)}, f32[2,128]{1,0:T(2,128)}) custom-call(bf16[4096,512]{1,0:T(8,128)(2,1)} %rec.1, bf16[32,128]{1,0:T(8,128)(2,1)} %bitcast.2, s32[32]{0:T(128)} %days.1, s32[32]{0:T(128)} %counts.1, f32[512,512]{1,0:T(8,128)} %prop_in.1, f32[512,512]{1,0:T(8,128)} %cov_in.1, f32[128,512]{1,0:T(8,128)} %kslab_in.1, f32[2,512]{1,0:T(2,128)} %damp.1, ...), custom_call_target="tpu_custom_call" | custom-call | flops 10000000000 | bytes 100000000 | tf_op jit(solution)/shard_map/pallas_call | solution.py:608
  143.1 1.2 shard_map.105

commit v6 on v4

--- a/solution.py
+++ b/solution.py
@@ -28,7 +28,7 @@
     return g * 8 + g // 2 * 4
 
 
-PARTS = (((0, 0, 512, 0), (3, 384, 128, 512)), ((1, 128, 384, 0), (2, 256, 256, 384)))
+PARTS = (((0, 0, 512, 0), (3, 384, 128, 512)), ((1, 128, 384, 0), (2, 384, 128, 384), (2, 256, 128, 512)))
 
 
 def row_times(ref, row):
@@ -265,7 +265,7 @@
 
     def first_copies(d, owner):
         return [remote(acc.at[pl.ds(d * 512 + 128 * r, 128), pl.ds(c0, w)], r1.at[d, :, pl.ds(at, w)],
-                       s_1.at[2 * d + n], r_1.at[2 * d + n], (sib, x))
+                       s_1.at[3 * d + n], r_1.at[3 * d + n], (sib, x))
                 for n, (r, c0, w, at) in enumerate(PARTS[owner])]
 
     def by_core(step):
@@ -289,8 +289,17 @@
     for copy in info_copies:
         copy.start()
         sent(copy)
-    second = [remote(hs.at[d], r2.at[d], s_2.at[d], r_2.at[d], (tm, xp)) for d in range(2)]
-    third = [remote(fh.at[d], r3.at[d], s_3.at[d], r_3.at[d], (sib, x)) for d in range(2)]
+    def pieces(src, dst, ss, rs, dev):
+        return [[remote(src.at[d, :, pl.ds(0, 512)], dst.at[d, :, pl.ds(0, 512)], ss.at[2 * d], rs.at[2 * d], dev),
+                 remote(src.at[d, pl.ds(0, 64), pl.ds(512, 128)], dst.at[d, pl.ds(0, 64), pl.ds(512, 128)],
+                        ss.at[2 * d + 1], rs.at[2 * d + 1], dev)] for d in range(2)]
+
+    second = pieces(hs, r2, s_2, r_2, (tm, xp))
+    third = pieces(fh, r3, s_3, r_3, (sib, x))
+    left = lax.broadcasted_iota(jnp.int32, (64, 128), 1) < 64
+    corner = jnp.logical_and(lax.broadcasted_iota(jnp.int32, (128, 128), 1) < 64,
+                             lax.broadcasted_iota(jnp.int32, (128, 128), 0) >= 64)
+
     for d in range(2):
         def add(own, d=d):
             for copy in first_copies(d, own):
@@ -300,8 +309,10 @@
                                        + r1[d, :, at:at + w])
 
         by_core(add)
-        second[d].start()
-        sent(second[d])
+        hs[d, 64:128, 0:128] = jnp.where(left, pltpu.roll(hs[d, 64:128, 512:640], 64, 1), hs[d, 64:128, 0:128])
+        for copy in second[d]:
+            copy.start()
+            sent(copy)
     for copy in info_copies:
         copy.wait_recv()
     info = (acc[1024:1032, :] + ri[0]) + (ri[1] + ri[2])
@@ -317,18 +328,28 @@
     wide[0:128, :] = prop[:, pl.ds(pl.multiple_of(j * 128, 128), 128)].T * d_rows[0:1, :]
     wide[128:136, :] = jnp.zeros((8, S), F32)
     for d in range(2):
-        second[d].wait_recv()
-        fh[d] = hs[d] + r2[d]
-        third[d].start()
-        sent(third[d])
+        for copy in second[d]:
+            copy.wait_recv()
+        fh[d, :, 0:512] = hs[d, :, 0:512] + r2[d, :, 0:512]
+        fh[d, 0:64, 512:640] = hs[d, 0:64, 512:640] + r2[d, 0:64, 512:640]
+        for copy in third[d]:
+            copy.start()
+            sent(copy)
         def put(own, src, d=d):
             for r, c0, w, at in PARTS[own]:
-                om[d, 128 * r:128 * r + 128, c0:c0 + w] = src[d, :, at:at + w]
+                if at < 512:
+                    om[d, 128 * r:128 * r + 128, c0:c0 + w] = src[d, :, at:at + w]
+                else:
+                    om[d, 128 * r:128 * r + 64, c0:c0 + w] = src[d, 0:64, at:at + w]
+                    om[d, 128 * r + 64:128 * r + 128, c0:c0 + w] = pltpu.roll(src[d, 64:128, 0:128], 64, 1)
 
         by_core(lambda own: put(own, fh))
-        third[d].wait_recv()
+        for copy in third[d]:
+            copy.wait_recv()
         by_core(lambda own: put(1 - own, r3))
-        for r in range(1, 4):
+        for r in range(4):
+            whole = om[d, 128 * r:128 * r + 128, 128 * r:128 * r + 128]
+            om[d, 128 * r:128 * r + 128, 128 * r:128 * r + 128] = jnp.where(corner, whole.T, whole)
             for c in range(r):
                 om[d, 128 * r:128 * r + 128, 128 * c:128 * c + 128] = (
                     om[d, 128 * c:128 * c + 128, 128 * r:128 * r + 128].T)
@@ -643,7 +664,7 @@
             pltpu.VMEM((4, S, 128), F32),
             dma((32,)), dma((32,)), dma((32,)), dma((32,)),
             dma((4,)), dma((4,)), dma((1,)), dma((1,)), dma((1,)), dma((4,)),
-            dma((4,)), dma((4,)), dma((3,)), dma((3,)), dma((2,)), dma((2,)), dma((2,)), dma((2,)),
+            dma((6,)), dma((6,)), dma((3,)), dma((3,)), dma((4,)), dma((4,)), dma((4,)), dma((4,)),
             dma((1,)), dma((32,)), dma((1,)), dma((8,)), dma((1,)), dma((1,)),
             dma((32,)), dma((1,)), dma((32,)), dma((32,)), dma,
             pltpu.VMEM((S, S), F32), pltpu.VMEM((S, S), F32), pltpu.VMEM((128, S), F32), dma((3,)),

time: 145 us -> 143 us (0.986)
  no operation moved by 1% of the time
where the time goes in v6:
time: 143 us
  Pallas kernels  143 us (100%)
    pallas_call x1, Pallas kernels, local(): pl.pallas_call(kernel, out_shape=(jax.ShapeDtypeStruct((2, 128), F32), ja...  141 us

profile of v6, /device:TPU:1, one launch (start us, length us, event | category | flops | bytes accessed | tf_op | source)
XLA Modules:
  0.0 143.3 jit_solution(3914712290482109417)
XLA Ops:
  0.6 141.4 %shard_map.104 = (f32[2,128]{1,0:T(2,128)}, f32[2,128]{1,0:T(2,128)}) custom-call(bf16[4096,512]{1,0:T(8,128)(2,1)} %rec.1, bf16[32,128]{1,0:T(8,128)(2,1)} %bitcast.2, s32[32]{0:T(128)} %days.1, s32[32]{0:T(128)} %counts.1, f32[512,512]{1,0:T(8,128)} %prop_in.1, f32[512,512]{1,0:T(8,128)} %cov_in.1, f32[128,512]{1,0:T(8,128)} %kslab_in.1, f32[2,512]{1,0:T(2,128)} %damp.1, ...), custom_call_target="tpu_custom_call" | custom-call | flops 10000000000 | bytes 100000000 | tf_op jit(solution)/shard_map/pallas_call | solution.py:626
  142.0 1.2 shard_map.105
